TPU v7x, 32 devices: a whole 2x2x4 slice. The times are simulated.
32 devices in a mesh: gx: 4 (over x, core), gy: 8 (over z, y).
Axes of the slice: x: 2, y: 2, z: 4, core: 2. Of those that a mesh axis runs over, the one named last changes fastest.
Arguments:
- fields: float32 [5, 192, 18432], P(None, 'gx', 'gy'), may hold values from -6 to 6
- winds: float32 [3, 192, 18432], P(None, 'gx', 'gy'), may hold values from -0.1 to 0.1
- diffusion: float32 [192, 18432], P('gx', 'gy'), may hold values from 0.02 to 0.06
- droplets: float32 [16384, 12, 128], P(('gx', 'gy')), may hold values from -3 to 3, as said below
- cells: int32 [16384, 128], P(('gx', 'gy')), may hold values from 0 to 110591, as said below
- balance_list: int32 [16384], P(('gx', 'gy')), may hold values from -1 to 8191, as said below
Outputs:
- fields_out: float32 [5, 192, 18432], P(None, 'gx', 'gy')
- droplets_out: float32 [8192, 12, 128], P(('gx', 'gy'))
Inputs may be any that keep to these rules, and one draw needn't show every extreme that they name: `droplets`: Rows: radius in 0.3 to 2, solute term in 0.003 to 0.03, weight in 0.5 to 2, positions and aerosol fractions in 0 to 1, velocities in -3 to 3. `cells`: A cell is (x * 48 + y) * 48 + z in the home tile. All 128 droplets of a block lie in one column (x, y), and within a block the cell never falls. `balance_list`: each home's used entries come first; every value from 0 to 8191 appears exactly once; at most 16 entries of one home name one owner, and some home uses all 512 entries.
All inputs are finite; a program needn't handle non-finite values.
Results may differ from a plain program's by a relative error of at most 0.00011.
Values sent between devices are 32-bit elements; how exact they have to be, the bound alone decides.
A program may use at most 128 MiB of HBM per device.

v0:
```python
import jax
import jax.numpy as jnp
from jax import lax
from jax.experimental import pallas as pl
from jax.experimental.pallas import tpu as pltpu
from jax.sharding import PartitionSpec as P

NZ = 48
OWN_BLK = 256
SUBSTEPS = 4
LANES = 128
ROW0 = 16
VMEM = pl.BlockSpec(memory_space=pltpu.VMEM)
SMEM = pl.BlockSpec(memory_space=pltpu.SMEM)
LIMIT = 56 * 1024 * 1024


def params():
    return pltpu.CompilerParams(vmem_limit_bytes=LIMIT)


def cost(bytes_accessed, flops):
    return pl.CostEstimate(flops=flops, bytes_accessed=bytes_accessed, transcendentals=0)


def send_kernel(home_cap, send_cap, rows, base_ref, live_ref, drops_ref, out_ref):
    def body(b, carry):
        block = drops_ref[pl.ds(home_cap + b, rows, stride=home_cap), :]
        out_ref[pl.ds(base_ref[b], rows, stride=send_cap), :] = block
        return carry

    lax.fori_loop(0, live_ref[0], body, 0)


def send_rows(base, live_count, planes, home_cap, send_cap):
    rows = planes.shape[0] // home_cap - 1
    return pl.pallas_call(
        lambda *refs: send_kernel(home_cap, send_cap, rows, *refs),
        out_shape=jax.ShapeDtypeStruct((rows * home_cap, LANES), jnp.float32),
        in_specs=[SMEM, SMEM, VMEM],
        out_specs=VMEM,
        compiler_params=params(),
        cost_estimate=cost(6 << 20, 1 << 20),
        name="send_rows",
    )(base, live_count, planes)


def grow_kernel(
    home_cap,
    column_ref,
    position_ref,
    live_ref,
    table_ref,
    level_ref,
    drops_ref,
    cond_ref,
    sent_ref,
    picked,
    radius_out,
    mass,
):
    live_count = live_ref[0]

    def fetch(g, carry):
        for i in range(8):
            b = g * 8 + i
            picked[pl.ds(b, 1), :] = table_ref[pl.ds(column_ref[b], 1), :]
        return carry

    lax.fori_loop(0, home_cap // 8, fetch, 0)

    def one(g, carry):
        at = pl.multiple_of(g * 8, 8)
        rows = pl.ds(at, 8)
        level = level_ref[rows, :]
        pair = picked[rows, :]
        theta = jnp.take_along_axis(pair, level, axis=1)
        vapour = jnp.take_along_axis(pair, level + 64, axis=1)
        supersat = vapour - 0.5 * jnp.tanh(theta)
        growth_rate = 1.0 / (1.0 + 0.1 * theta * theta)
        start = drops_ref[rows, :]
        solute = drops_ref[pl.ds(home_cap + at, 8), :]
        weight = drops_ref[pl.ds(2 * home_cap + at, 8), :]
        square = start * start
        for _ in range(SUBSTEPS):
            radius = jnp.sqrt(square)
            square = jnp.maximum(
                square
                + 0.05
                * growth_rate
                * (supersat - 0.02 / radius + solute / (radius * radius * radius)),
                0.04,
            )
        radius = jnp.sqrt(square)
        radius_out[rows, :] = radius
        grown = weight * (radius * square - start * start * start)
        block = at + lax.broadcasted_iota(jnp.int32, (8, LANES), 0)
        mass[rows, :] = jnp.where(block < live_count, grown, 0.0)
        return carry

    lax.fori_loop(0, home_cap // 8, one, 0)

    def send(b, carry):
        sent_ref[pl.ds(position_ref[b], 1), :] = radius_out[pl.ds(b, 1), :]
        return carry

    lax.fori_loop(0, live_count, send, 0)
    row = lax.broadcasted_iota(jnp.int32, (LANES, LANES), 0)
    column = lax.broadcasted_iota(jnp.int32, (LANES, LANES), 1)
    upper = (row <= column).astype(jnp.float32)
    mass[...] = jnp.dot(
        mass[...], upper, precision=lax.Precision.HIGHEST, preferred_element_type=jnp.float32
    )
    cond_ref[...] = jnp.zeros_like(cond_ref)
    lane = lax.broadcasted_iota(jnp.int32, (8, LANES), 1)

    def sums(g, carry):
        rows = pl.ds(pl.multiple_of(g * 8, 8), 8)
        level = level_ref[rows, :]
        count = jnp.zeros((8, LANES), jnp.int32)
        step = LANES
        while step >= 1:
            probe = jnp.minimum(count + (step - 1), LANES - 1)
            below = jnp.take_along_axis(level, probe, axis=1) <= lane
            count = jnp.where(below & (count + step <= LANES), count + step, count)
            step //= 2
        upto = jnp.take_along_axis(mass[rows, :], jnp.maximum(count - 1, 0), axis=1)
        upto = jnp.where(count > 0, upto, 0.0)
        before = jnp.where(lane == 0, 0.0, pltpu.roll(upto, 1, 1))
        picked[rows, :] = upto - before
        return carry

    lax.fori_loop(0, home_cap // 8, sums, 0)

    def scatter(b, carry):
        at = pl.ds(column_ref[b], 1)
        cond_ref[at, :] = cond_ref[at, :] + picked[pl.ds(b, 1), :]
        return carry

    lax.fori_loop(0, live_count, scatter, 0)


def grow_blocks(column, position, live_count, table, level, planes):
    home_cap = level.shape[0]
    scratch = pltpu.VMEM((home_cap, LANES), jnp.float32)
    return pl.pallas_call(
        lambda *refs: grow_kernel(home_cap, *refs),
        out_shape=(
            jax.ShapeDtypeStruct(table.shape, jnp.float32),
            jax.ShapeDtypeStruct((home_cap, LANES), jnp.float32),
        ),
        in_specs=[SMEM, SMEM, SMEM, VMEM, VMEM, VMEM],
        out_specs=(VMEM, VMEM),
        scratch_shapes=[scratch, scratch, scratch],
        compiler_params=params(),
        cost_estimate=cost(8 << 20, 1 << 24),
        name="grow_blocks",
    )(column, position, live_count, table, level, planes)


def place_kernel(home_cap, send_cap, rows, source_ref, radius_ref, arrived_ref, out_ref):
    per_device = rows * send_cap

    def body(g, carry):
        for i in range(8):
            j = g * 8 + i
            source = source_ref[j]
            first = (source // send_cap) * per_device + source % send_cap
            block = arrived_ref[pl.ds(first, rows, stride=send_cap), :]
            out_ref[pl.ds(OWN_BLK + j, rows, stride=OWN_BLK), :] = block
            out_ref[pl.ds(j, 1), :] = radius_ref[pl.ds(source, 1), :]
        return carry

    lax.fori_loop(0, OWN_BLK // 8, body, 0)
    for r in range(3, 6):
        at = pl.ds(r * OWN_BLK, OWN_BLK)
        out_ref[at, :] = out_ref[at, :] + 0.1 * out_ref[pl.ds((r + 3) * OWN_BLK, OWN_BLK), :]


def place_blocks(source, radius, arrived, send_cap):
    home_cap = radius.shape[0]
    rows = arrived.shape[0] // home_cap
    return pl.pallas_call(
        lambda *refs: place_kernel(home_cap, send_cap, rows, *refs),
        out_shape=jax.ShapeDtypeStruct(((rows + 1) * OWN_BLK, LANES), jnp.float32),
        in_specs=[SMEM, VMEM, VMEM],
        out_specs=VMEM,
        compiler_params=params(),
        cost_estimate=cost(5 << 20, 1 << 20),
        name="place_blocks",
    )(source, radius, arrived)


def stencil_kernel(
    fields_ref,
    winds_ref,
    diff_ref,
    low_x,
    high_x,
    low_y,
    high_y,
    cond_ref,
    out_ref,
    ext,
    mid,
    coef,
):
    width = fields_ref.shape[1]
    merged = fields_ref.shape[2]
    lanes = merged + 2 * LANES
    core = slice(LANES, LANES + merged)
    inner = slice(ROW0, ROW0 + width)
    for k in range(9):
        if k < 5:
            own = fields_ref[k]
        elif k < 8:
            own = winds_ref[k - 5]
        else:
            own = diff_ref[...]
        ext[k, inner, core] = own
        ext[k, ROW0 - 2 : ROW0, core] = low_x[k]
        ext[k, ROW0 + width : ROW0 + width + 2, core] = high_x[k]
        ext[k, ROW0 - 2 : ROW0 + width + 2, 0:LANES] = low_y[k]
        ext[k, ROW0 - 2 : ROW0 + width + 2, LANES + merged : lanes] = high_y[k]

    chunks = range(ROW0 - 8, ROW0 + width + 8, 8)
    z = (lax.broadcasted_iota(jnp.int32, (8, lanes), 1) + (NZ - LANES % NZ)) % NZ
    top = z == NZ - 1
    bottom = z == 0

    def faces(c_low, c_high, k_low, k_high):
        courant = 0.5 * (c_low + c_high)
        diffuse = 0.5 * (k_low + k_high)
        return jnp.maximum(courant, 0.0) + diffuse, jnp.minimum(courant, 0.0) - diffuse

    def ahead(v, n):
        return pltpu.roll(v, lanes - n, 1)

    def behind(v, n):
        return pltpu.roll(v, n, 1)

    for base in chunks:
        rows = slice(base, base + 8)
        up = slice(base + 1, base + 9)
        down = slice(base - 1, base + 7)
        k0 = ext[8, rows, :]
        u0 = ext[5, rows, :]
        p, n = faces(u0, ext[5, up, :], k0, ext[8, up, :])
        p_low, n_low = faces(ext[5, down, :], u0, ext[8, down, :], k0)
        centre = 1.0 - (p - n_low)
        coef[0, rows, :] = -n
        coef[1, rows, :] = p_low
        v0 = ext[6, rows, :]
        p, n = faces(v0, ahead(v0, NZ), k0, ahead(k0, NZ))
        centre = centre - (p - behind(n, NZ))
        coef[2, rows, :] = -n
        coef[3, rows, :] = behind(p, NZ)
        w0 = ext[7, rows, :]
        p, n = faces(w0, ahead(w0, 1), k0, ahead(k0, 1))
        p = jnp.where(top, 0.0, p)
        n = jnp.where(top, 0.0, n)
        coef[4, rows, :] = -n
        p_low = jnp.where(bottom, 0.0, behind(p, 1))
        n_low = jnp.where(bottom, 0.0, behind(n, 1))
        coef[5, rows, :] = p_low
        coef[6, rows, :] = centre - (p - n_low)

    def update(src, f, base):
        rows = slice(base, base + 8)
        mine = src[f, rows, :]
        new = coef[6, rows, :] * mine
        new += coef[0, rows, :] * src[f, base + 1 : base + 9, :]
        new += coef[1, rows, :] * src[f, base - 1 : base + 7, :]
        new += coef[2, rows, :] * ahead(mine, NZ)
        new += coef[3, rows, :] * behind(mine, NZ)
        new += coef[4, rows, :] * ahead(mine, 1)
        new += coef[5, rows, :] * behind(mine, 1)
        return new

    def first(f, carry):
        for base in chunks:
            mid[f, base : base + 8, :] = update(ext, f, base)
        return carry

    lax.fori_loop(0, 5, first, 0)

    def second(f, carry):
        share = jnp.where(f == 0, 0.25, jnp.where(f == 1, -0.1, 0.0))
        for base in range(ROW0, ROW0 + width, 8):
            at = slice(base - ROW0, base - ROW0 + 8)
            out_ref[f, at, :] = update(mid, f, base)[:, core] + share * cond_ref[at, :]
        return carry

    lax.fori_loop(0, 5, second, 0)


def advance(fields, winds, diffusion, low_x, high_x, low_y, high_y, condensed):
    _, width, merged = fields.shape
    tall = ROW0 + width + 16
    wide = merged + 2 * LANES
    return pl.pallas_call(
        stencil_kernel,
        out_shape=jax.ShapeDtypeStruct(fields.shape, jnp.float32),
        in_specs=[VMEM] * 8,
        out_specs=VMEM,
        scratch_shapes=[
            pltpu.VMEM((9, tall, wide), jnp.float32),
            pltpu.VMEM((5, tall, wide), jnp.float32),
            pltpu.VMEM((7, tall, wide), jnp.float32),
        ],
        compiler_params=params(),
        cost_estimate=cost(16 << 20, 1 << 26),
        name="advance",
    )(fields, winds, diffusion, low_x, high_x, low_y, high_y, condensed)


def both_ways(low_edge, high_edge, axis):
    count = lax.axis_size(axis)
    return (
        lax.ppermute(high_edge, axis, [(i, (i + 1) % count) for i in range(count)]),
        lax.ppermute(low_edge, axis, [((i + 1) % count, i) for i in range(count)]),
    )


def per_device(fields, winds, diffusion, droplets, cells, balance_list):
    width = fields.shape[1]
    merged = fields.shape[2]
    home_cap = balance_list.shape[0]
    devices = lax.axis_size(("gx", "gy"))
    send_cap = home_cap // devices
    rows = droplets.shape[1] - 1
    column_count = width * merged // NZ

    def edge(xs, ys):
        grids = (fields, winds, diffusion[None])
        return jnp.concatenate([g[:, xs, ys] for g in grids], axis=0)

    every = slice(None)
    low_x, high_x = both_ways(
        edge(slice(0, 2), every), edge(slice(width - 2, width), every), "gx"
    )
    strip = 2 * NZ

    def side(ys):
        return jnp.concatenate([low_x[:, :, ys], edge(every, ys), high_x[:, :, ys]], axis=1)

    low_y, high_y = both_ways(side(slice(0, strip)), side(slice(merged - strip, merged)), "gy")
    low_y = jnp.pad(low_y, ((0, 0), (0, 0), (LANES - strip, 0)))
    high_y = jnp.pad(high_y, ((0, 0), (0, 0), (0, LANES - strip)))

    live = balance_list >= 0
    owner = jnp.where(live, balance_list // OWN_BLK, devices)
    slot = balance_list % OWN_BLK
    order = lax.iota(jnp.int32, home_cap)
    earlier = (owner[:, None] == owner[None, :]) & (order[None, :] < order[:, None])
    rank = jnp.sum(earlier.astype(jnp.int32), axis=1)
    position = jnp.where(live, owner * send_cap + rank, home_cap)
    base = jnp.where(live, owner * (send_cap * rows) + rank, 0)
    live_count = jnp.sum(live.astype(jnp.int32))[None]
    codes = (
        jnp.sum(
            jnp.where(position[None, :] == order[:, None], slot[None, :] + 1, 0), axis=1
        )
        - 1
    )
    planes = droplets.transpose(1, 0, 2).reshape((rows + 1) * home_cap, LANES)
    everyone = ("gx", "gy")

    def exchange(x):
        return lax.all_to_all(x, everyone, split_axis=0, concat_axis=0, tiled=True)

    arrived_codes = exchange(codes.reshape(devices, send_cap)).reshape(-1)
    outgoing = send_rows(base, live_count, planes, home_cap, send_cap)
    arrived = exchange(outgoing)

    level = cells % NZ
    column = cells[:, 0] // NZ
    gap = jnp.zeros((column_count, LANES // 2 - NZ), jnp.float32)
    table = jnp.concatenate(
        [
            fields[0].reshape(column_count, NZ),
            gap,
            fields[1].reshape(column_count, NZ),
            gap,
        ],
        axis=1,
    )
    condensed, radius = grow_blocks(column, position, live_count, table, level, planes)
    arrived_radius = exchange(radius)
    condensed = condensed[:, :NZ].reshape(width, merged)
    fields_out = advance(fields, winds, diffusion, low_x, high_x, low_y, high_y, condensed)

    own = lax.iota(jnp.int32, OWN_BLK)
    source = jnp.sum(
        jnp.where(arrived_codes[None, :] == own[:, None], order[None, :], 0), axis=1
    )
    placed = place_blocks(source, arrived_radius, arrived, send_cap)
    droplets_out = placed.reshape(rows + 1, OWN_BLK, LANES).transpose(1, 0, 2)
    return (fields_out, droplets_out)


def solution(mesh):
    return jax.shard_map(
        per_device,
        mesh=mesh,
        in_specs=(
            P(None, "gx", "gy"),
            P(None, "gx", "gy"),
            P("gx", "gy"),
            P(("gx", "gy"), None, None),
            P(("gx", "gy"), None),
            P(("gx", "gy")),
        ),
        out_specs=(P(None, "gx", "gy"), P(("gx", "gy"), None, None)),
        check_vma=False,
    )
```

profile of v0, /device:TPU:19, one launch (start us, length us, event | category | flops | bytes accessed | tf_op | source)
XLA Modules:
  0.0 198.5 jit_solution(6223940208568674535)
XLA Ops:
  0.6 1.1 copy.12
  1.7 1.4 convert_reduce_fusion.1
  3.1 0.7 fusion.1
  3.8 0.3 convert_reduce_fusion
  4.1 0.6 add_select_fusion.4
  4.7 0.2 select_reduce_fusion
  4.9 0.7 sub.19
  5.6 6.2 %all-to-all-start = ((s32[32,1,16]{2,1,0:T(1,128)}), s32[32,1,16]{2,1,0:T(1,128)S(1)}, u32[]{:S(2)}, u32[]{:S(2)}) async-start(s32[32,1,16]{2,1,0:T(1,128)} %bitcast.5), calls=%async_computation | async-start | bytes 32768 | tf_op jit(solution)/shard_map/all_to_all | solution.py:370
  11.8 1.2 fusion.4
  13.0 0.7 reshape_squeeze.6
  13.7 0.7 reshape_squeeze.7
  14.5 0.1 broadcast_in_dim.57
  14.6 2.0 %pad_maximum_fusion.refs_3_ = f32[2304,128]{1,0:T(8,128)} fusion(f32[2304,16]{1,0:T(8,128)S(1)} %broadcast_in_dim.57, f32[2304,48]{1,0:T(8,128)S(1)} %reshape_squeeze.7, f32[2304,48]{1,0:T(8,128)S(1)} %reshape_squeeze.6), kind=kLoop, calls=%fused_computation | loop fusion | flops 884736 | bytes 2211840 | tf_op jit(solution)/shard_map/concatenate | solution.py:379
  16.6 0.8 add_select_fusion.refs_4_
  17.4 62.7 %grow_blocks.1 = (f32[2304,128]{1,0:T(8,128)}, f32[512,128]{1,0:T(8,128)}) custom-call(s32[512]{0:T(512)} %get-tuple-element.29.refs_0_, s32[512]{0:T(512)} %copy-done.5, s32[1]{0:T(128)} %bitcast.2.refs_2_.refs_1_, f32[2304,128]{1,0:T(8,128)} %pad_maximum_fusion.refs_3_, s32[512,128]{1,0:T(8,128)} %add_select_fusion.refs_4_, f32[6144,128]{1,0:T(8,128)} %bitcast.16), custom_call_target="tpu_custom_call" | custom-call | flops 16777216 | bytes 8388608 | tf_op jit(solution)/shard_map/grow_blocks/pallas_call | solution.py:146
  80.2 10.5 %all-to-all-start.1 = ((f32[32,16,128]{2,1,0:T(8,128)}), f32[32,16,128]{2,1,0:T(8,128)S(1)}, u32[]{:S(2)}, u32[]{:S(2)}) async-start(f32[32,16,128]{2,1,0:T(8,128)} %bitcast.26), calls=%async_computation.1 | async-start | bytes 524288 | tf_op jit(solution)/shard_map/all_to_all | solution.py:370
  90.6 4.5 %send_rows.1 = f32[5632,128]{1,0:T(8,128)} custom-call(s32[512]{0:T(512)} %get-tuple-element.26.refs_0_, s32[1]{0:T(128)} %bitcast.2.refs_2_.refs_1_, f32[6144,128]{1,0:T(8,128)} %bitcast.17), custom_call_target="tpu_custom_call" | custom-call | flops 1048576 | bytes 6291456 | tf_op jit(solution)/shard_map/send_rows/pallas_call | solution.py:37
  95.2 2.9 %all-to-all-done.1 = f32[32,16,128]{2,1,0:T(8,128)S(1)} async-done(((f32[32,16,128]{2,1,0:T(8,128)}), f32[32,16,128]{2,1,0:T(8,128)S(1)}, u32[]{:S(2)}, u32[]{:S(2)}) %all-to-all-start.1) | async-done | bytes 262176 | tf_op jit(solution)/shard_map/all_to_all | solution.py:370
  98.1 0.7 copy-done.1
  98.8 7.1 %all-to-all-start.2 = ((f32[32,176,128]{2,1,0:T(8,128)}), f32[32,176,128]{2,1,0:T(8,128)S(1)}, u32[]{:S(2)}, u32[]{:S(2)}) async-start(f32[32,176,128]{2,1,0:T(8,128)} %bitcast.18), calls=%async_computation.2 | async-start | bytes 5767168 | tf_op jit(solution)/shard_map/all_to_all | solution.py:370
  105.9 0.9 fusion.10
  106.8 1.1 fusion.8
  107.9 1.2 fusion.6
  109.1 0.1 pad_maximum_fusion.3
  109.2 0.6 collective-permute-start
  109.8 0.1 pad_maximum_fusion.4
  109.9 0.1 collective-permute-start.1
  109.9 1.0 fusion.7
  110.9 1.1 fusion.5
  112.0 0.8 fusion.9
  112.8 12.9 %collective-permute-done.low_x = f32[9,2,2304]{2,1,0:T(2,128)S(1)} collective-permute-done((f32[9,2,2304]{2,1,0:T(2,128)S(1)}, f32[9,2,2304]{2,1,0:T(2,128)S(1)}, u32[]{:S(2)}, u32[]{:S(2)}) %collective-permute-start) | collective-permute-done | bytes 165920 | tf_op jit(solution)/shard_map/ppermute | solution.py:320
  125.8 0.1 fusion.11
  125.8 3.4 %collective-permute-done.1.high_x = f32[9,2,2304]{2,1,0:T(2,128)S(1)} collective-permute-done((f32[9,2,2304]{2,1,0:T(2,128)S(1)}, f32[9,2,2304]{2,1,0:T(2,128)S(1)}, u32[]{:S(2)}, u32[]{:S(2)}) %collective-permute-start.1) | collective-permute-done | bytes 165920 | tf_op jit(solution)/shard_map/ppermute | solution.py:321
  129.3 0.1 fusion.12
  129.3 0.7 pad_maximum_fusion.1
  130.1 0.7 pad_maximum_fusion.2
  130.8 2.4 %collective-permute-start.3 = (f32[9,52,96]{2,1,0:T(8,128)}, f32[9,52,96]{2,1,0:T(8,128)S(1)}, u32[]{:S(2)}, u32[]{:S(2)}) collective-permute-start(f32[9,52,96]{2,1,0:T(8,128)} %pad_maximum_fusion.2), channel_id=1, source_target_pairs={{1,0},{2,1},{3,2},{4,3},{5,4},{6,5},{7,6},{0,7},{9,8},{10,9},{11,1... | collective-permute-start | bytes 539144 | tf_op jit(solution)/shard_map/ppermute | solution.py:321
  133.2 2.5 %reshape.51.cond_ref = f32[48,2304]{1,0:T(8,128)} reshape(f32[2304,48]{1,0:T(8,128)} %bitcast.21) | data formatting | bytes 884736 | tf_op jit(solution)/shard_map/reshape | solution.py:390
  135.7 0.5 broadcast.49
  136.2 0.7 reduce.5
  136.9 0.1 eq.48
  137.0 0.7 select_reduce_fusion.1.refs_0_
  137.6 38.5 %collective-permute-done.2 = f32[9,52,96]{2,1,0:T(8,128)S(1)} collective-permute-done((f32[9,52,96]{2,1,0:T(8,128)}, f32[9,52,96]{2,1,0:T(8,128)S(1)}, u32[]{:S(2)}, u32[]{:S(2)}) %collective-permute-start.2) | collective-permute-done | bytes 179744 | tf_op jit(solution)/shard_map/ppermute | solution.py:320
  176.1 0.8 pad.8.low_y
  177.0 0.7 pad.9.high_y
  177.7 13.5 %advance.1 = f32[5,48,2304]{2,1,0:T(8,128)} custom-call(f32[5,48,2304]{2,1,0:T(8,128)} %fields_ref.1, f32[3,48,2304]{2,1,0:T(8,128)} %winds_ref.1, f32[48,2304]{1,0:T(8,128)} %diff_ref.1, f32[9,2,2304]{2,1,0:T(2,128)} %copy-done.3, f32[9,2,2304]{2,1,0:T(2,128)} %copy-done.4, f32[9,52,128]{2,1,0:T(8,128)} %pad.8.low_y, f32[9,52,128]{2,1,0:T(8,128)} %pad.9.high_y, ...), custom_call_target="tpu_custom_call" | custom-call | flops 67108864 | bytes 16777216 | tf_op jit(solution)/shard_map/advance/pallas_call | solution.py:301
  191.2 1.6 copy-done
  192.8 5.8 %place_blocks.1 = f32[3072,128]{1,0:T(8,128)} custom-call(s32[256]{0:T(256)} %select_reduce_fusion.1.refs_0_, f32[512,128]{1,0:T(8,128)} %bitcast.22, f32[5632,128]{1,0:T(8,128)} %bitcast.19), custom_call_target="tpu_custom_call" | custom-call | flops 1048576 | bytes 5242880 | tf_op jit(solution)/shard_map/place_blocks/pallas_call | solution.py:183
  (17 shorter events, 0.1 us)
Async XLA Ops:
  4.7 9.0 %copy-start.5 = (s32[512]{0:T(512)}, s32[512]{0:T(512)S(1)}, u32[]{:S(2)}) copy-start(s32[512]{0:T(512)S(1)} %get-tuple-element.27.refs_1_) | copy-start | bytes 6148
  5.6 74.6 %all-to-all-start = ((s32[32,1,16]{2,1,0:T(1,128)}), s32[32,1,16]{2,1,0:T(1,128)S(1)}, u32[]{:S(2)}, u32[]{:S(2)}) async-start(s32[32,1,16]{2,1,0:T(1,128)} %bitcast.5), calls=%async_computation | async-start | bytes 32768 | tf_op jit(solution)/shard_map/all_to_all | solution.py:370
  14.5 2.0 %copy-start.2 = (s32[512,128]{1,0:T(8,128)S(1)}, s32[512,128]{1,0:T(8,128)}, u32[]{:S(2)}) copy-start(s32[512,128]{1,0:T(8,128)} %param.10) | copy-start | bytes 786436
  80.2 17.9 %all-to-all-start.1 = ((f32[32,16,128]{2,1,0:T(8,128)}), f32[32,16,128]{2,1,0:T(8,128)S(1)}, u32[]{:S(2)}, u32[]{:S(2)}) async-start(f32[32,16,128]{2,1,0:T(8,128)} %bitcast.26), calls=%async_computation.1 | async-start | bytes 524288 | tf_op jit(solution)/shard_map/all_to_all | solution.py:370
  98.1 0.7 copy-start.1
  98.8 92.4 %all-to-all-start.2 = ((f32[32,176,128]{2,1,0:T(8,128)}), f32[32,176,128]{2,1,0:T(8,128)S(1)}, u32[]{:S(2)}, u32[]{:S(2)}) async-start(f32[32,176,128]{2,1,0:T(8,128)} %bitcast.18), calls=%async_computation.2 | async-start | bytes 5767168 | tf_op jit(solution)/shard_map/all_to_all | solution.py:370
  109.2 16.6 %collective-permute-start = (f32[9,2,2304]{2,1,0:T(2,128)S(1)}, f32[9,2,2304]{2,1,0:T(2,128)S(1)}, u32[]{:S(2)}, u32[]{:S(2)}) collective-permute-start(f32[9,2,2304]{2,1,0:T(2,128)S(1)} %pad_maximum_fusion.3), channel_id=1, source_target_pairs={{0,8},{8,16},{16,24},{24,0},{1,9},{9,17},{17,25},{25,1},{2,10},{10... | collective-permute-start | bytes 497672 | tf_op jit(solution)/shard_map/ppermute | solution.py:320
  109.9 19.4 %collective-permute-start.1 = (f32[9,2,2304]{2,1,0:T(2,128)S(1)}, f32[9,2,2304]{2,1,0:T(2,128)S(1)}, u32[]{:S(2)}, u32[]{:S(2)}) collective-permute-start(f32[9,2,2304]{2,1,0:T(2,128)S(1)} %pad_maximum_fusion.4), channel_id=1, source_target_pairs={{8,0},{16,8},{24,16},{0,24},{9,1},{17,9},{25,17},{1,25},{10,2},{18... | collective-permute-start | bytes 497672 | tf_op jit(solution)/shard_map/ppermute | solution.py:321
  125.8 5.1 %copy-start.3 = (f32[9,2,2304]{2,1,0:T(2,128)}, f32[9,2,2304]{2,1,0:T(2,128)S(1)}, u32[]{:S(2)}) copy-start(f32[9,2,2304]{2,1,0:T(2,128)S(1)} %collective-permute-done.low_x) | copy-start | bytes 497668
  129.3 3.9 %copy-start.4 = (f32[9,2,2304]{2,1,0:T(2,128)}, f32[9,2,2304]{2,1,0:T(2,128)S(1)}, u32[]{:S(2)}) copy-start(f32[9,2,2304]{2,1,0:T(2,128)S(1)} %collective-permute-done.1.high_x) | copy-start | bytes 497668
  130.1 46.1 %collective-permute-start.2 = (f32[9,52,96]{2,1,0:T(8,128)}, f32[9,52,96]{2,1,0:T(8,128)S(1)}, u32[]{:S(2)}, u32[]{:S(2)}) collective-permute-start(f32[9,52,96]{2,1,0:T(8,128)} %pad_maximum_fusion.1), channel_id=1, source_target_pairs={{0,1},{1,2},{2,3},{3,4},{4,5},{5,6},{6,7},{7,0},{8,9},{9,10},{10,1... | collective-permute-start | bytes 539144 | tf_op jit(solution)/shard_map/ppermute | solution.py:320
  130.8 46.2 %collective-permute-start.3 = (f32[9,52,96]{2,1,0:T(8,128)}, f32[9,52,96]{2,1,0:T(8,128)S(1)}, u32[]{:S(2)}, u32[]{:S(2)}) collective-permute-start(f32[9,52,96]{2,1,0:T(8,128)} %pad_maximum_fusion.2), channel_id=1, source_target_pairs={{1,0},{2,1},{3,2},{4,3},{5,4},{6,5},{7,6},{0,7},{9,8},{10,9},{11,1... | collective-permute-start | bytes 539144 | tf_op jit(solution)/shard_map/ppermute | solution.py:321
  191.2 1.6 copy-start
where the time goes:
time: 198 us; the launch traced here: 199 us
  Pallas kernels  86.5 us (44%)
  waiting for transfers between devices  57.8 us (29%)
  starting transfers between devices  26.8 us (14%)
  local copies, waits for them, and re-layouts  17.7 us (9%)
  other arithmetic  9 us (5%)
    pallas_call x1, Pallas kernels, grow_blocks(): pl.pallas_call(lambda *refs: grow_kernel(home_cap, *refs), out_shape=(jax...  62.7 us
    ppermute x2, waiting for transfers between devices, both_ways(): lax.ppermute(high_edge, axis, [(i, (i + 1) % count) for i in range(count)])  51.4 us
    all_to_all x3, starting transfers between devices, exchange(): return lax.all_to_all(x, everyone, split_axis=0, concat_axis=0, tiled=True)  23.8 us
    pallas_call x1, Pallas kernels, advance(): pl.pallas_call(stencil_kernel, out_shape=jax.ShapeDtypeStruct(fields.shap...  13.5 us
    slice x6, local copies, waits for them, and re-layouts, edge(): return jnp.concatenate([g[:, xs, ys] for g in grids], axis=0)  6.08 us
    pallas_call x1, Pallas kernels, place_blocks(): pl.pallas_call(lambda *refs: place_kernel(home_cap, send_cap, rows, *refs...  5.76 us
    pallas_call x1, Pallas kernels, send_rows(): pl.pallas_call(lambda *refs: send_kernel(home_cap, send_cap, rows, *refs)...  4.55 us
  transfers between devices with their start and end apart: 7, of which 4 were waited for; matrix products, arithmetic and copies ran while one was open for 10% of the time, Pallas kernels for 41%

commit v1 on v0

--- a/solution.py
+++ b/solution.py
@@ -10,6 +10,7 @@
 SUBSTEPS = 4
 LANES = 128
 ROW0 = 16
+BATCH = 64
 VMEM = pl.BlockSpec(memory_space=pltpu.VMEM)
 SMEM = pl.BlockSpec(memory_space=pltpu.SMEM)
 LIMIT = 56 * 1024 * 1024
@@ -23,32 +24,50 @@
     return pl.CostEstimate(flops=flops, bytes_accessed=bytes_accessed, transcendentals=0)
 
 
-def send_kernel(home_cap, send_cap, rows, base_ref, live_ref, drops_ref, out_ref):
-    def body(b, carry):
-        block = drops_ref[pl.ds(home_cap + b, rows, stride=home_cap), :]
-        out_ref[pl.ds(base_ref[b], rows, stride=send_cap), :] = block
-        return carry
-
-    lax.fori_loop(0, live_ref[0], body, 0)
-
-
-def send_rows(base, live_count, planes, home_cap, send_cap):
+CODE_ROWS = 8
+
+
+def send_kernel(home_cap, send_cap, rows, source_ref, code_ref, drops_ref, out_ref):
+    devices = home_cap // send_cap
+    per_device = rows * send_cap + CODE_ROWS
+    unroll = min(8, send_cap)
+
+    def body(g, carry):
+        start = (g // (send_cap // unroll)) * per_device + (g % (send_cap // unroll)) * unroll
+        for i in range(unroll):
+            b = source_ref[g * unroll + i]
+            block = drops_ref[pl.ds(home_cap + b, rows, stride=home_cap), :]
+            out_ref[pl.ds(start + i, rows, stride=send_cap), :] = block
+        return carry
+
+    lax.fori_loop(0, home_cap // unroll, body, 0)
+
+    def codes(d, carry):
+        out_ref[pl.ds(d * per_device + rows * send_cap, 1), :] = code_ref[pl.ds(d, 1), :]
+        return carry
+
+    lax.fori_loop(0, devices, codes, 0)
+
+
+def send_rows(source, codes, planes, home_cap, send_cap):
     rows = planes.shape[0] // home_cap - 1
+    devices = home_cap // send_cap
+    total = devices * (rows * send_cap + CODE_ROWS)
     return pl.pallas_call(
         lambda *refs: send_kernel(home_cap, send_cap, rows, *refs),
-        out_shape=jax.ShapeDtypeStruct((rows * home_cap, LANES), jnp.float32),
-        in_specs=[SMEM, SMEM, VMEM],
+        out_shape=jax.ShapeDtypeStruct((total, LANES), jnp.float32),
+        in_specs=[SMEM, VMEM, VMEM],
         out_specs=VMEM,
         compiler_params=params(),
         cost_estimate=cost(6 << 20, 1 << 20),
         name="send_rows",
-    )(base, live_count, planes)
+    )(source, codes, planes)
 
 
 def grow_kernel(
     home_cap,
     column_ref,
-    position_ref,
+    source_ref,
     live_ref,
     table_ref,
     level_ref,
@@ -70,8 +89,8 @@
     lax.fori_loop(0, home_cap // 8, fetch, 0)
 
     def one(g, carry):
-        at = pl.multiple_of(g * 8, 8)
-        rows = pl.ds(at, 8)
+        at = pl.multiple_of(g * BATCH, BATCH)
+        rows = pl.ds(at, BATCH)
         level = level_ref[rows, :]
         pair = picked[rows, :]
         theta = jnp.take_along_axis(pair, level, axis=1)
@@ -79,8 +98,8 @@
         supersat = vapour - 0.5 * jnp.tanh(theta)
         growth_rate = 1.0 / (1.0 + 0.1 * theta * theta)
         start = drops_ref[rows, :]
-        solute = drops_ref[pl.ds(home_cap + at, 8), :]
-        weight = drops_ref[pl.ds(2 * home_cap + at, 8), :]
+        solute = drops_ref[pl.ds(home_cap + at, BATCH), :]
+        weight = drops_ref[pl.ds(2 * home_cap + at, BATCH), :]
         square = start * start
         for _ in range(SUBSTEPS):
             radius = jnp.sqrt(square)
@@ -94,17 +113,19 @@
         radius = jnp.sqrt(square)
         radius_out[rows, :] = radius
         grown = weight * (radius * square - start * start * start)
-        block = at + lax.broadcasted_iota(jnp.int32, (8, LANES), 0)
+        block = at + lax.broadcasted_iota(jnp.int32, (BATCH, LANES), 0)
         mass[rows, :] = jnp.where(block < live_count, grown, 0.0)
         return carry
 
-    lax.fori_loop(0, home_cap // 8, one, 0)
-
-    def send(b, carry):
-        sent_ref[pl.ds(position_ref[b], 1), :] = radius_out[pl.ds(b, 1), :]
-        return carry
-
-    lax.fori_loop(0, live_count, send, 0)
+    lax.fori_loop(0, home_cap // BATCH, one, 0)
+
+    def send(g, carry):
+        for i in range(8):
+            b = g * 8 + i
+            sent_ref[pl.ds(b, 1), :] = radius_out[pl.ds(source_ref[b], 1), :]
+        return carry
+
+    lax.fori_loop(0, home_cap // 8, send, 0)
     row = lax.broadcasted_iota(jnp.int32, (LANES, LANES), 0)
     column = lax.broadcasted_iota(jnp.int32, (LANES, LANES), 1)
     upper = (row <= column).astype(jnp.float32)
@@ -112,12 +133,12 @@
         mass[...], upper, precision=lax.Precision.HIGHEST, preferred_element_type=jnp.float32
     )
     cond_ref[...] = jnp.zeros_like(cond_ref)
-    lane = lax.broadcasted_iota(jnp.int32, (8, LANES), 1)
+    lane = lax.broadcasted_iota(jnp.int32, (BATCH, LANES), 1)
 
     def sums(g, carry):
-        rows = pl.ds(pl.multiple_of(g * 8, 8), 8)
+        rows = pl.ds(pl.multiple_of(g * BATCH, BATCH), BATCH)
         level = level_ref[rows, :]
-        count = jnp.zeros((8, LANES), jnp.int32)
+        count = jnp.zeros((BATCH, LANES), jnp.int32)
         step = LANES
         while step >= 1:
             probe = jnp.minimum(count + (step - 1), LANES - 1)
@@ -130,17 +151,19 @@
         picked[rows, :] = upto - before
         return carry
 
-    lax.fori_loop(0, home_cap // 8, sums, 0)
-
-    def scatter(b, carry):
-        at = pl.ds(column_ref[b], 1)
-        cond_ref[at, :] = cond_ref[at, :] + picked[pl.ds(b, 1), :]
-        return carry
-
-    lax.fori_loop(0, live_count, scatter, 0)
-
-
-def grow_blocks(column, position, live_count, table, level, planes):
+    lax.fori_loop(0, home_cap // BATCH, sums, 0)
+
+    def scatter(g, carry):
+        for i in range(8):
+            b = g * 8 + i
+            at = pl.ds(column_ref[b], 1)
+            cond_ref[at, :] = cond_ref[at, :] + picked[pl.ds(b, 1), :]
+        return carry
+
+    lax.fori_loop(0, home_cap // 8, scatter, 0)
+
+
+def grow_blocks(column, source, live_count, table, level, planes):
     home_cap = level.shape[0]
     scratch = pltpu.VMEM((home_cap, LANES), jnp.float32)
     return pl.pallas_call(
@@ -155,11 +178,11 @@
         compiler_params=params(),
         cost_estimate=cost(8 << 20, 1 << 24),
         name="grow_blocks",
-    )(column, position, live_count, table, level, planes)
-
-
-def place_kernel(home_cap, send_cap, rows, source_ref, radius_ref, arrived_ref, out_ref):
-    per_device = rows * send_cap
+    )(column, source, live_count, table, level, planes)
+
+
+def place_kernel(home_cap, send_cap, rows, source_ref, arrived_ref, out_ref):
+    per_device = rows * send_cap + CODE_ROWS
 
     def body(g, carry):
         for i in range(8):
@@ -168,7 +191,6 @@
             first = (source // send_cap) * per_device + source % send_cap
             block = arrived_ref[pl.ds(first, rows, stride=send_cap), :]
             out_ref[pl.ds(OWN_BLK + j, rows, stride=OWN_BLK), :] = block
-            out_ref[pl.ds(j, 1), :] = radius_ref[pl.ds(source, 1), :]
         return carry
 
     lax.fori_loop(0, OWN_BLK // 8, body, 0)
@@ -177,18 +199,43 @@
         out_ref[at, :] = out_ref[at, :] + 0.1 * out_ref[pl.ds((r + 3) * OWN_BLK, OWN_BLK), :]
 
 
-def place_blocks(source, radius, arrived, send_cap):
-    home_cap = radius.shape[0]
-    rows = arrived.shape[0] // home_cap
+def place_blocks(source, arrived, home_cap, send_cap, rows):
     return pl.pallas_call(
         lambda *refs: place_kernel(home_cap, send_cap, rows, *refs),
         out_shape=jax.ShapeDtypeStruct(((rows + 1) * OWN_BLK, LANES), jnp.float32),
-        in_specs=[SMEM, VMEM, VMEM],
+        in_specs=[SMEM, VMEM],
         out_specs=VMEM,
         compiler_params=params(),
         cost_estimate=cost(5 << 20, 1 << 20),
         name="place_blocks",
-    )(source, radius, arrived)
+    )(source, arrived)
+
+
+def place_radius_kernel(source_ref, radius_ref, placed_ref, out_ref, rows_ref, sem):
+    def body(g, carry):
+        for i in range(8):
+            j = g * 8 + i
+            rows_ref[pl.ds(j, 1), :] = radius_ref[pl.ds(source_ref[j], 1), :]
+        return carry
+
+    lax.fori_loop(0, OWN_BLK // 8, body, 0)
+    copy = pltpu.make_async_copy(rows_ref, out_ref.at[pl.ds(0, OWN_BLK), :], sem)
+    copy.start()
+    copy.wait()
+
+
+def place_radius(source, radius, placed):
+    return pl.pallas_call(
+        place_radius_kernel,
+        out_shape=jax.ShapeDtypeStruct(placed.shape, jnp.float32),
+        in_specs=[SMEM, VMEM, pl.BlockSpec(memory_space=pl.ANY)],
+        out_specs=pl.BlockSpec(memory_space=pl.ANY),
+        scratch_shapes=[pltpu.VMEM((OWN_BLK, LANES), jnp.float32), pltpu.SemaphoreType.DMA],
+        input_output_aliases={2: 0},
+        compiler_params=params(),
+        cost_estimate=cost(1 << 19, 1 << 16),
+        name="place_radius",
+    )(source, radius, placed)
 
 
 def stencil_kernel(
@@ -336,17 +383,10 @@
         return jnp.concatenate([g[:, xs, ys] for g in grids], axis=0)
 
     every = slice(None)
-    low_x, high_x = both_ways(
-        edge(slice(0, 2), every), edge(slice(width - 2, width), every), "gx"
-    )
+    x_edges = (edge(slice(0, 2), every), edge(slice(width - 2, width), every))
+    x_edges, balance_list = lax.optimization_barrier((x_edges, balance_list))
+    low_x, high_x = both_ways(*x_edges, "gx")
     strip = 2 * NZ
-
-    def side(ys):
-        return jnp.concatenate([low_x[:, :, ys], edge(every, ys), high_x[:, :, ys]], axis=1)
-
-    low_y, high_y = both_ways(side(slice(0, strip)), side(slice(merged - strip, merged)), "gy")
-    low_y = jnp.pad(low_y, ((0, 0), (0, 0), (LANES - strip, 0)))
-    high_y = jnp.pad(high_y, ((0, 0), (0, 0), (0, LANES - strip)))
 
     live = balance_list >= 0
     owner = jnp.where(live, balance_list // OWN_BLK, devices)
@@ -355,26 +395,34 @@
     earlier = (owner[:, None] == owner[None, :]) & (order[None, :] < order[:, None])
     rank = jnp.sum(earlier.astype(jnp.int32), axis=1)
     position = jnp.where(live, owner * send_cap + rank, home_cap)
-    base = jnp.where(live, owner * (send_cap * rows) + rank, 0)
     live_count = jnp.sum(live.astype(jnp.int32))[None]
-    codes = (
-        jnp.sum(
-            jnp.where(position[None, :] == order[:, None], slot[None, :] + 1, 0), axis=1
-        )
-        - 1
-    )
+    taken = position[None, :] == order[:, None]
+    send_source = jnp.sum(jnp.where(taken, order[None, :], 0), axis=1)
+    codes = jnp.sum(jnp.where(taken, slot[None, :] + 1, 0), axis=1) - 1
+    codes = codes.astype(jnp.float32).reshape(devices, send_cap)
+    codes = jnp.pad(codes, ((0, 0), (0, LANES - send_cap)))
     planes = droplets.transpose(1, 0, 2).reshape((rows + 1) * home_cap, LANES)
     everyone = ("gx", "gy")
 
+    def side(ys):
+        return jnp.concatenate([low_x[:, :, ys], edge(every, ys), high_x[:, :, ys]], axis=1)
+
+    sides = (side(slice(0, strip)), side(slice(merged - strip, merged)))
+    sides, send_source = lax.optimization_barrier((sides, send_source))
+    low_y, high_y = both_ways(*sides, "gy")
+
     def exchange(x):
         return lax.all_to_all(x, everyone, split_axis=0, concat_axis=0, tiled=True)
 
-    arrived_codes = exchange(codes.reshape(devices, send_cap)).reshape(-1)
-    outgoing = send_rows(base, live_count, planes, home_cap, send_cap)
+    outgoing = send_rows(send_source, codes, planes, home_cap, send_cap)
+    outgoing, low_y, high_y, column = lax.optimization_barrier(
+        (outgoing, low_y, high_y, cells[:, 0] // NZ)
+    )
     arrived = exchange(outgoing)
+    low_y = jnp.pad(low_y, ((0, 0), (0, 0), (LANES - strip, 0)))
+    high_y = jnp.pad(high_y, ((0, 0), (0, 0), (0, LANES - strip)))
 
     level = cells % NZ
-    column = cells[:, 0] // NZ
     gap = jnp.zeros((column_count, LANES // 2 - NZ), jnp.float32)
     table = jnp.concatenate(
         [
@@ -385,16 +433,22 @@
         ],
         axis=1,
     )
-    condensed, radius = grow_blocks(column, position, live_count, table, level, planes)
-    arrived_radius = exchange(radius)
+    condensed, radius = grow_blocks(column, send_source, live_count, table, level, planes)
     condensed = condensed[:, :NZ].reshape(width, merged)
     fields_out = advance(fields, winds, diffusion, low_x, high_x, low_y, high_y, condensed)
 
-    own = lax.iota(jnp.int32, OWN_BLK)
+    arrived, radius, fields_out = lax.optimization_barrier((arrived, radius, fields_out))
+    arrived_radius = exchange(radius)
+    per_device_rows = arrived.shape[0] // devices
+    arrived_codes = arrived.reshape(devices, per_device_rows, LANES)[
+        :, rows * send_cap, :send_cap
+    ].reshape(-1)
+    own = lax.iota(jnp.int32, OWN_BLK).astype(jnp.float32)
     source = jnp.sum(
         jnp.where(arrived_codes[None, :] == own[:, None], order[None, :], 0), axis=1
     )
-    placed = place_blocks(source, arrived_radius, arrived, send_cap)
+    placed = place_blocks(source, arrived, home_cap, send_cap, rows)
+    placed = place_radius(source, arrived_radius, placed)
     droplets_out = placed.reshape(rows + 1, OWN_BLK, LANES).transpose(1, 0, 2)
     return (fields_out, droplets_out)
 

time: 198 us -> 119 us (0.60)
  the two profiles are of different devices: /device:TPU:19 before, /device:TPU:0 now
where the time goes in v1:
time: 119 us; the launch traced here: 118 us
  Pallas kernels  43.7 us (37%)
  waiting for transfers between devices  30 us (25%)
  local copies, waits for them, and re-layouts  20.4 us (17%)
  starting transfers between devices  14.3 us (12%)
  other arithmetic  8.68 us (7%)
    all_to_all x2, waiting for transfers between devices, exchange(): return lax.all_to_all(x, everyone, split_axis=0, concat_axis=0, tiled=True)  27.9 us
    pallas_call x1, Pallas kernels, grow_blocks(): pl.pallas_call(lambda *refs: grow_kernel(home_cap, *refs), out_shape=(jax...  15.2 us
    pallas_call x1, Pallas kernels, advance(): pl.pallas_call(stencil_kernel, out_shape=jax.ShapeDtypeStruct(fields.shap...  13.5 us
    pallas_call x1, Pallas kernels, send_rows(): pl.pallas_call(lambda *refs: send_kernel(home_cap, send_cap, rows, *refs)...  7.5 us
    all_to_all x2, starting transfers between devices, exchange(): return lax.all_to_all(x, everyone, split_axis=0, concat_axis=0, tiled=True)  6.31 us
    slice x6, local copies, waits for them, and re-layouts, edge(): return jnp.concatenate([g[:, xs, ys] for g in grids], axis=0)  6.12 us
    pallas_call x1, Pallas kernels, place_blocks(): pl.pallas_call(lambda *refs: place_kernel(home_cap, send_cap, rows, *refs...  5.56 us
    ppermute x2, starting transfers between devices, both_ways(): lax.ppermute(low_edge, axis, [((i + 1) % count, i) for i in range(count)])  5.08 us
  transfers between devices with their start and end apart: 6, of which 3 were waited for; matrix products, arithmetic and copies ran while one was open for 21% of the time, Pallas kernels for 35%

profile of v1, /device:TPU:0, one launch (start us, length us, event | category | flops | bytes accessed | tf_op | source)
XLA Modules:
  0.0 117.8 jit_solution(11246260932096469252)
XLA Ops:
  0.6 0.0 copy-start.3
  0.6 1.0 fusion.10
  1.6 0.0 copy-start.6
  1.6 1.1 fusion.8
  2.7 1.2 fusion.6
  3.9 0.2 pad_maximum_fusion.3
  4.1 0.5 collective-permute-start
  4.6 2.0 %collective-permute-start.1 = (f32[9,2,2304]{2,1,0:T(2,128)S(1)}, f32[9,2,2304]{2,1,0:T(2,128)S(1)}, u32[]{:S(2)}, u32[]{:S(2)}) collective-permute-start(f32[9,2,2304]{2,1,0:T(2,128)S(1)} %get-tuple-element.18), channel_id=1, source_target_pairs={{8,0},{16,8},{24,16},{0,24},{9,1},{17,9},{25,17},{1,25},{10,2},{18... | collective-permute-start | bytes 497672 | tf_op jit(solution)/shard_map/ppermute | solution.py:368
  6.6 0.8 fusion.9
  7.4 1.0 fusion.7
  8.4 1.1 fusion.5
  9.5 0.1 copy.13
  9.6 0.0 copy-done.6
  9.6 0.7 convert_reduce_fusion.1
  10.3 0.2 convert_reduce_fusion
  10.6 1.0 select_reduce_fusion
  11.6 0.1 convert_element_type.28
  11.7 0.6 pad.12.refs_1_
  12.3 0.0 collective-permute-done.low_x
  12.3 0.1 fusion.11
  12.4 0.0 collective-permute-done.1.high_x
  12.4 0.1 fusion.12
  12.6 2.3 %collective-permute-start.2 = (f32[9,52,96]{2,1,0:T(8,128)S(1)}, f32[9,52,96]{2,1,0:T(8,128)}, u32[]{:S(2)}, u32[]{:S(2)}) collective-permute-start(f32[9,52,96]{2,1,0:T(8,128)S(1)} %pad_maximum_fusion.2), channel_id=1, source_target_pairs={{0,1},{1,2},{2,3},{3,4},{4,5},{5,6},{6,7},{7,0},{8,9},{9,10},{10,1... | collective-permute-start | bytes 539144 | tf_op jit(solution)/shard_map/ppermute | solution.py:367
  14.9 3.1 %collective-permute-start.3 = (f32[9,52,96]{2,1,0:T(8,128)S(1)}, f32[9,52,96]{2,1,0:T(8,128)}, u32[]{:S(2)}, u32[]{:S(2)}) collective-permute-start(f32[9,52,96]{2,1,0:T(8,128)S(1)} %pad_maximum_fusion.1), channel_id=1, source_target_pairs={{1,0},{2,1},{3,2},{4,3},{5,4},{6,5},{7,6},{0,7},{9,8},{10,9},{11,1... | collective-permute-start | bytes 539144 | tf_op jit(solution)/shard_map/ppermute | solution.py:368
  18.0 0.6 add_select_fusion.1.refs_0_
  18.6 7.5 %send_rows.1 = f32[5888,128]{1,0:T(8,128)} custom-call(s32[512]{0:T(512)} %get-tuple-element.20.refs_0_.refs_1_, f32[32,128]{1,0:T(8,128)} %pad.12.refs_1_, f32[6144,128]{1,0:T(8,128)} %bitcast.19), custom_call_target="tpu_custom_call" | custom-call | flops 1048576 | bytes 6291456 | tf_op jit(solution)/shard_map/send_rows/pallas_call | solution.py:56
  26.1 0.0 collective-permute-done.2
  26.1 2.1 %collective-permute-done.3 = f32[9,52,96]{2,1,0:T(8,128)} collective-permute-done((f32[9,52,96]{2,1,0:T(8,128)S(1)}, f32[9,52,96]{2,1,0:T(8,128)}, u32[]{:S(2)}, u32[]{:S(2)}) %collective-permute-start.3) | collective-permute-done | bytes 179744 | tf_op jit(solution)/shard_map/ppermute | solution.py:368
  28.3 3.7 %all-to-all-start = ((f32[32,184,128]{2,1,0:T(8,128)}), f32[32,184,128]{2,1,0:T(8,128)S(1)}, u32[]{:S(2)}, u32[]{:S(2)}) async-start(f32[32,184,128]{2,1,0:T(8,128)} %bitcast.22), calls=%async_computation | async-start | bytes 6029312 | tf_op jit(solution)/shard_map/all_to_all | solution.py:415
  31.9 2.0 %fusion.4 = (f32[1,48,2304]{2,1,0:T(8,128)}, f32[1,48,2304]{2,1,0:T(8,128)S(1)}) fusion(f32[5,48,2304]{2,1,0:T(8,128)} %fields_ref.1), kind=kLoop, calls=%fused_computation.31 | loop fusion | bytes 1769472 | tf_op jit(solution)/shard_map/slice | solution.py:429
  33.9 2.8 %reshape_squeeze.6 = f32[2304,48]{1,0:T(8,128)} reshape(f32[1,48,2304]{2,1,0:T(8,128)} %get-tuple-element.34) | data formatting | bytes 884736 | tf_op jit(solution)/shard_map/reshape;squeeze | solution.py:429
  36.7 1.8 %reshape_squeeze.7 = f32[2304,48]{1,0:T(8,128)} reshape(f32[1,48,2304]{2,1,0:T(8,128)S(1)} %get-tuple-element.35) | data formatting | bytes 884736 | tf_op jit(solution)/shard_map/reshape;squeeze | solution.py:431
  38.4 1.9 %add_select_fusion.refs_4_ = s32[512,128]{1,0:T(8,128)} fusion(s32[512,128]{1,0:T(8,128)} %param.10), kind=kLoop, calls=%fused_computation.8 | loop fusion | flops 393216 | bytes 524288 | tf_op jit(solution)/shard_map/jit(remainder)/select_n | solution.py:425
  40.3 0.1 broadcast_in_dim.63
  40.4 3.3 %pad_maximum_fusion.refs_3_ = f32[2304,128]{1,0:T(8,128)} fusion(f32[2304,16]{1,0:T(8,128)S(1)} %broadcast_in_dim.63, f32[2304,48]{1,0:T(8,128)} %reshape_squeeze.7, f32[2304,48]{1,0:T(8,128)S(1)} %copy-done.1), kind=kLoop, calls=%fused_computation | loop fusion | flops 884736 | bytes 2211840 | tf_op jit(solution)/shard_map/concatenate | solution.py:427
  43.7 15.2 %grow_blocks.1 = (f32[2304,128]{1,0:T(8,128)}, f32[512,128]{1,0:T(8,128)}) custom-call(s32[512]{0:T(512)} %add_select_fusion.1.refs_0_, s32[512]{0:T(512)} %get-tuple-element.20.refs_0_.refs_1_, s32[1]{0:T(128)} %bitcast.6.refs_2_, f32[2304,128]{1,0:T(8,128)} %pad_maximum_fusion.refs_3_, s32[512,128]{1,0:T(8,128)} %add_select_fusion.refs_4_, ...), custom_call_target="tpu_custom_call" | custom-call | flops 16777216 | bytes 8388608 | tf_op jit(solution)/shard_map/grow_blocks/pallas_call | solution.py:169
  58.8 2.5 %reshape.46.cond_ref = f32[48,2304]{1,0:T(8,128)} reshape(f32[2304,48]{1,0:T(8,128)} %bitcast.24) | data formatting | bytes 884736 | tf_op jit(solution)/shard_map/reshape | solution.py:437
  61.3 1.8 %pad.13.low_y = f32[9,52,128]{2,1,0:T(8,128)} pad(f32[9,52,96]{2,1,0:T(8,128)} %collective-permute-done.2, f32[]{:T(128)} %constant.55.clone.1), padding=0_0x0_0x32_0 | pad | bytes 419332 | tf_op jit(solution)/shard_map/jit(_pad)/pad | solution.py:422
  63.1 1.6 %pad.14.high_y = f32[9,52,128]{2,1,0:T(8,128)} pad(f32[9,52,96]{2,1,0:T(8,128)} %collective-permute-done.3, f32[]{:T(128)} %constant.55.clone.1), padding=0_0x0_0x0_32 | pad | bytes 419332 | tf_op jit(solution)/shard_map/jit(_pad)/pad | solution.py:423
  64.7 13.5 %advance.1 = f32[5,48,2304]{2,1,0:T(8,128)} custom-call(f32[5,48,2304]{2,1,0:T(8,128)} %fields_ref.1, f32[3,48,2304]{2,1,0:T(8,128)} %winds_ref.1, f32[48,2304]{1,0:T(8,128)} %diff_ref.1, f32[9,2,2304]{2,1,0:T(2,128)} %copy-done.4, f32[9,2,2304]{2,1,0:T(2,128)} %copy-done.5, f32[9,52,128]{2,1,0:T(8,128)} %pad.13.low_y, f32[9,52,128]{2,1,0:T(8,128)} %pad.14.high_y, ...), custom_call_target="tpu_custom_call" | custom-call | flops 67108864 | bytes 16777216 | tf_op jit(solution)/shard_map/advance/pallas_call | solution.py:348
  78.2 23.9 %all-to-all-done = f32[32,184,128]{2,1,0:T(8,128)S(1)} async-done(((f32[32,184,128]{2,1,0:T(8,128)}), f32[32,184,128]{2,1,0:T(8,128)S(1)}, u32[]{:S(2)}, u32[]{:S(2)}) %all-to-all-start) | async-done | bytes 3014688 | tf_op jit(solution)/shard_map/all_to_all | solution.py:415
  102.1 2.6 %all-to-all-start.1 = ((f32[32,16,128]{2,1,0:T(8,128)}), f32[32,16,128]{2,1,0:T(8,128)S(1)}, u32[]{:S(2)}, u32[]{:S(2)}) async-start(f32[32,16,128]{2,1,0:T(8,128)} %bitcast.9), calls=%async_computation.1 | async-start | bytes 524288 | tf_op jit(solution)/shard_map/all_to_all | solution.py:415
  104.7 0.1 eq.48
  104.8 0.7 select_reduce_fusion.2.refs_0_.source_ref
  105.5 5.6 %place_blocks.1.placed_ref = f32[3072,128]{1,0:T(8,128)} custom-call(s32[256]{0:T(256)} %select_reduce_fusion.2.refs_0_.source_ref, f32[5888,128]{1,0:T(8,128)} %bitcast.21), custom_call_target="tpu_custom_call" | custom-call | flops 1048576 | bytes 5242880 | tf_op jit(solution)/shard_map/place_blocks/pallas_call | solution.py:203
  111.1 4.0 %all-to-all-done.1 = f32[32,16,128]{2,1,0:T(8,128)S(1)} async-done(((f32[32,16,128]{2,1,0:T(8,128)}), f32[32,16,128]{2,1,0:T(8,128)S(1)}, u32[]{:S(2)}, u32[]{:S(2)}) %all-to-all-start.1) | async-done | bytes 262176 | tf_op jit(solution)/shard_map/all_to_all | solution.py:415
  115.1 0.7 copy-done.2
  115.8 2.0 %place_radius.1 = f32[3072,128]{1,0:T(8,128)} custom-call(s32[256]{0:T(256)} %select_reduce_fusion.2.refs_0_.source_ref, f32[512,128]{1,0:T(8,128)} %bitcast.25, f32[3072,128]{1,0:T(8,128)} %place_blocks.1.placed_ref), custom_call_target="tpu_custom_call", output_to_operand_aliasing={{}: (2, {})} | custom-call | flops 65536 | bytes 524288 | tf_op jit(solution)/shard_map/place_radius/pallas_call | solution.py:228
  (18 shorter events, 0.2 us)
Async XLA Ops:
  0.6 8.9 %copy-start.3 = (s32[512,128]{1,0:T(8,128)S(1)}, s32[512,128]{1,0:T(8,128)}, u32[]{:S(2)}) copy-start(s32[512,128]{1,0:T(8,128)} %param.10) | copy-start | bytes 786436
  1.6 8.0 %copy-start.6 = (s32[512]{0:T(512)S(1)}, s32[512]{0:T(512)}, u32[]{:S(2)}) copy-start(s32[512]{0:T(512)} %param.11) | copy-start | bytes 6148
  4.1 8.2 %collective-permute-start = (f32[9,2,2304]{2,1,0:T(2,128)S(1)}, f32[9,2,2304]{2,1,0:T(2,128)S(1)}, u32[]{:S(2)}, u32[]{:S(2)}) collective-permute-start(f32[9,2,2304]{2,1,0:T(2,128)S(1)} %get-tuple-element.17), channel_id=1, source_target_pairs={{0,8},{8,16},{16,24},{24,0},{1,9},{9,17},{17,25},{25,1},{2,10},{10... | collective-permute-start | bytes 497672 | tf_op jit(solution)/shard_map/ppermute | solution.py:367
  4.6 7.8 %collective-permute-start.1 = (f32[9,2,2304]{2,1,0:T(2,128)S(1)}, f32[9,2,2304]{2,1,0:T(2,128)S(1)}, u32[]{:S(2)}, u32[]{:S(2)}) collective-permute-start(f32[9,2,2304]{2,1,0:T(2,128)S(1)} %get-tuple-element.18), channel_id=1, source_target_pairs={{8,0},{16,8},{24,16},{0,24},{9,1},{17,9},{25,17},{1,25},{10,2},{18... | collective-permute-start | bytes 497672 | tf_op jit(solution)/shard_map/ppermute | solution.py:368
  12.3 13.8 %copy-start.4 = (f32[9,2,2304]{2,1,0:T(2,128)}, f32[9,2,2304]{2,1,0:T(2,128)S(1)}, u32[]{:S(2)}) copy-start(f32[9,2,2304]{2,1,0:T(2,128)S(1)} %collective-permute-done.low_x) | copy-start | bytes 497668
  12.4 13.7 %copy-start.5 = (f32[9,2,2304]{2,1,0:T(2,128)}, f32[9,2,2304]{2,1,0:T(2,128)S(1)}, u32[]{:S(2)}) copy-start(f32[9,2,2304]{2,1,0:T(2,128)S(1)} %collective-permute-done.1.high_x) | copy-start | bytes 497668
  12.6 13.5 %collective-permute-start.2 = (f32[9,52,96]{2,1,0:T(8,128)S(1)}, f32[9,52,96]{2,1,0:T(8,128)}, u32[]{:S(2)}, u32[]{:S(2)}) collective-permute-start(f32[9,52,96]{2,1,0:T(8,128)S(1)} %pad_maximum_fusion.2), channel_id=1, source_target_pairs={{0,1},{1,2},{2,3},{3,4},{4,5},{5,6},{6,7},{7,0},{8,9},{9,10},{10,1... | collective-permute-start | bytes 539144 | tf_op jit(solution)/shard_map/ppermute | solution.py:367
  14.9 13.3 %collective-permute-start.3 = (f32[9,52,96]{2,1,0:T(8,128)S(1)}, f32[9,52,96]{2,1,0:T(8,128)}, u32[]{:S(2)}, u32[]{:S(2)}) collective-permute-start(f32[9,52,96]{2,1,0:T(8,128)S(1)} %pad_maximum_fusion.1), channel_id=1, source_target_pairs={{1,0},{2,1},{3,2},{4,3},{5,4},{6,5},{7,6},{0,7},{9,8},{10,9},{11,1... | collective-permute-start | bytes 539144 | tf_op jit(solution)/shard_map/ppermute | solution.py:368
  28.3 73.8 %all-to-all-start = ((f32[32,184,128]{2,1,0:T(8,128)}), f32[32,184,128]{2,1,0:T(8,128)S(1)}, u32[]{:S(2)}, u32[]{:S(2)}) async-start(f32[32,184,128]{2,1,0:T(8,128)} %bitcast.22), calls=%async_computation | async-start | bytes 6029312 | tf_op jit(solution)/shard_map/all_to_all | solution.py:415
  38.4 2.0 %copy-start.1 = (f32[2304,48]{1,0:T(8,128)S(1)}, f32[2304,48]{1,0:T(8,128)}, u32[]{:S(2)}) copy-start(f32[2304,48]{1,0:T(8,128)} %reshape_squeeze.6) | copy-start | bytes 1327108
  102.1 3.5 %copy-start = (f32[32,184,128]{2,1,0:T(8,128)}, f32[32,184,128]{2,1,0:T(8,128)S(1)}, u32[]{:S(2)}) copy-start(f32[32,184,128]{2,1,0:T(8,128)S(1)} %all-to-all-done) | copy-start | bytes 9043972
  102.1 13.1 %all-to-all-start.1 = ((f32[32,16,128]{2,1,0:T(8,128)}), f32[32,16,128]{2,1,0:T(8,128)S(1)}, u32[]{:S(2)}, u32[]{:S(2)}) async-start(f32[32,16,128]{2,1,0:T(8,128)} %bitcast.9), calls=%async_computation.1 | async-start | bytes 524288 | tf_op jit(solution)/shard_map/all_to_all | solution.py:415
  115.1 0.7 copy-start.2

commit v2 on v1

--- a/solution.py
+++ b/solution.py
@@ -27,37 +27,34 @@
 CODE_ROWS = 8
 
 
-def send_kernel(home_cap, send_cap, rows, source_ref, code_ref, drops_ref, out_ref):
-    devices = home_cap // send_cap
+def send_kernel(home_cap, send_cap, rows, steps, source_ref, code_ref, drops_ref, out_ref):
+    devices = home_cap // send_cap // steps
     per_device = rows * send_cap + CODE_ROWS
-    unroll = min(8, send_cap)
-
-    def body(g, carry):
-        start = (g // (send_cap // unroll)) * per_device + (g % (send_cap // unroll)) * unroll
-        for i in range(unroll):
-            b = source_ref[g * unroll + i]
+    first = pl.program_id(0) * devices
+
+    def body(d, carry):
+        start = d * per_device
+        for i in range(send_cap):
+            b = source_ref[(first + d) * send_cap + i]
             block = drops_ref[pl.ds(home_cap + b, rows, stride=home_cap), :]
             out_ref[pl.ds(start + i, rows, stride=send_cap), :] = block
-        return carry
-
-    lax.fori_loop(0, home_cap // unroll, body, 0)
-
-    def codes(d, carry):
-        out_ref[pl.ds(d * per_device + rows * send_cap, 1), :] = code_ref[pl.ds(d, 1), :]
-        return carry
-
-    lax.fori_loop(0, devices, codes, 0)
+        out_ref[pl.ds(start + rows * send_cap, 1), :] = code_ref[pl.ds(first + d, 1), :]
+        return carry
+
+    lax.fori_loop(0, devices, body, 0)
 
 
 def send_rows(source, codes, planes, home_cap, send_cap):
     rows = planes.shape[0] // home_cap - 1
     devices = home_cap // send_cap
     total = devices * (rows * send_cap + CODE_ROWS)
+    steps = 4
     return pl.pallas_call(
-        lambda *refs: send_kernel(home_cap, send_cap, rows, *refs),
+        lambda *refs: send_kernel(home_cap, send_cap, rows, steps, *refs),
+        grid=(steps,),
         out_shape=jax.ShapeDtypeStruct((total, LANES), jnp.float32),
         in_specs=[SMEM, VMEM, VMEM],
-        out_specs=VMEM,
+        out_specs=pl.BlockSpec((total // steps, LANES), lambda i: (i, 0)),
         compiler_params=params(),
         cost_estimate=cost(6 << 20, 1 << 20),
         name="send_rows",
@@ -378,16 +375,8 @@
     rows = droplets.shape[1] - 1
     column_count = width * merged // NZ
 
-    def edge(xs, ys):
-        grids = (fields, winds, diffusion[None])
-        return jnp.concatenate([g[:, xs, ys] for g in grids], axis=0)
-
     every = slice(None)
-    x_edges = (edge(slice(0, 2), every), edge(slice(width - 2, width), every))
-    x_edges, balance_list = lax.optimization_barrier((x_edges, balance_list))
-    low_x, high_x = both_ways(*x_edges, "gx")
     strip = 2 * NZ
-
     live = balance_list >= 0
     owner = jnp.where(live, balance_list // OWN_BLK, devices)
     slot = balance_list % OWN_BLK
@@ -404,21 +393,29 @@
     planes = droplets.transpose(1, 0, 2).reshape((rows + 1) * home_cap, LANES)
     everyone = ("gx", "gy")
 
+    def exchange(x):
+        return lax.all_to_all(x, everyone, split_axis=0, concat_axis=0, tiled=True)
+
+    outgoing = send_rows(send_source, codes, planes, home_cap, send_cap)
+    outgoing, fields, winds, diffusion, cells = lax.optimization_barrier(
+        (outgoing, fields, winds, diffusion, cells)
+    )
+    arrived = exchange(outgoing)
+
+    def edge(xs, ys):
+        grids = (fields, winds, diffusion[None])
+        return jnp.concatenate([g[:, xs, ys] for g in grids], axis=0)
+
+    low_x, high_x = both_ways(
+        edge(slice(0, 2), every), edge(slice(width - 2, width), every), "gx"
+    )
+
     def side(ys):
         return jnp.concatenate([low_x[:, :, ys], edge(every, ys), high_x[:, :, ys]], axis=1)
 
     sides = (side(slice(0, strip)), side(slice(merged - strip, merged)))
-    sides, send_source = lax.optimization_barrier((sides, send_source))
+    sides, column = lax.optimization_barrier((sides, cells[:, 0] // NZ))
     low_y, high_y = both_ways(*sides, "gy")
-
-    def exchange(x):
-        return lax.all_to_all(x, everyone, split_axis=0, concat_axis=0, tiled=True)
-
-    outgoing = send_rows(send_source, codes, planes, home_cap, send_cap)
-    outgoing, low_y, high_y, column = lax.optimization_barrier(
-        (outgoing, low_y, high_y, cells[:, 0] // NZ)
-    )
-    arrived = exchange(outgoing)
     low_y = jnp.pad(low_y, ((0, 0), (0, 0), (LANES - strip, 0)))
     high_y = jnp.pad(high_y, ((0, 0), (0, 0), (0, LANES - strip)))
 

time: 119 us -> 124 us (1.042)
  starting transfers between devices: 14.3 us -> 35.1 us
  waiting for transfers between devices: 30 us -> 12 us
  other arithmetic: 8.68 us -> 12.7 us
  Pallas kernels: 43.7 us -> 42.3 us
    all_to_all x2, waiting for transfers between devices: 27.9 us -> 4.13 us  [exchange(): return lax.all_to_all(x, everyone, split_axis=0, concat_axis=0, tiled=True)]
    all_to_all x2, starting transfers between devices: 6.31 us -> 23.9 us  [exchange(): return lax.all_to_all(x, everyone, split_axis=0, concat_axis=0, tiled=True)]
    ppermute x2, waiting for transfers between devices: 0.01 us -> 7.17 us  [both_ways(): lax.ppermute(high_edge, axis, [(i, (i + 1) % count) for i in range(count)])]
    ppermute x2, starting transfers between devices: 2.87 us -> 4.98 us  [both_ways(): lax.ppermute(high_edge, axis, [(i, (i + 1) % count) for i in range(count)])]
    ppermute x2, waiting for transfers between devices: 2.13 us -> 0.65 us  [both_ways(): lax.ppermute(low_edge, axis, [((i + 1) % count, i) for i in range(count)])]
    concatenate x1 -> x2, other arithmetic: 0.16 us -> 1.47 us  [edge(): return jnp.concatenate([g[:, xs, ys] for g in grids], axis=0)]
    pallas_call x1, Pallas kernels: 7.5 us -> 6.2 us  [send_rows(): pl.pallas_call(lambda *refs: send_kernel(home_cap, send_cap, rows, steps,...]
  transfers between devices with their start and end apart: 6 -> 6, of which waited for: 3 -> 5; matrix products, arithmetic and copies ran while one was open for 21% -> 23% of each run, Pallas kernels for 35% -> 28%
where the time goes in v2:
time: 124 us
  Pallas kernels  42.3 us (34%)
  starting transfers between devices  35.1 us (28%)
  local copies, waits for them, and re-layouts  20.6 us (17%)
  other arithmetic  12.7 us (10%)
  waiting for transfers between devices  12 us (10%)
    all_to_all x2, starting transfers between devices, exchange(): return lax.all_to_all(x, everyone, split_axis=0, concat_axis=0, tiled=True)  23.9 us
    pallas_call x1, Pallas kernels, grow_blocks(): pl.pallas_call(lambda *refs: grow_kernel(home_cap, *refs), out_shape=(jax...  15.1 us
    pallas_call x1, Pallas kernels, advance(): pl.pallas_call(stencil_kernel, out_shape=jax.ShapeDtypeStruct(fields.shap...  13.5 us
    ppermute x2, waiting for transfers between devices, both_ways(): lax.ppermute(high_edge, axis, [(i, (i + 1) % count) for i in range(count)])  7.17 us
    ppermute x2, starting transfers between devices, both_ways(): lax.ppermute(low_edge, axis, [((i + 1) % count, i) for i in range(count)])  6.23 us
    pallas_call x1, Pallas kernels, send_rows(): pl.pallas_call(lambda *refs: send_kernel(home_cap, send_cap, rows, steps,...  6.2 us
    slice x6, local copies, waits for them, and re-layouts, edge(): return jnp.concatenate([g[:, xs, ys] for g in grids], axis=0)  6.12 us
    pallas_call x1, Pallas kernels, place_blocks(): pl.pallas_call(lambda *refs: place_kernel(home_cap, send_cap, rows, *refs...  5.56 us
  transfers between devices with their start and end apart: 6, of which 5 were waited for; matrix products, arithmetic and copies ran while one was open for 23% of the time, Pallas kernels for 28%

profile of v2, /device:TPU:0, one launch (start us, length us, event | category | flops | bytes accessed | tf_op | source)
XLA Modules:
  0.0 123.5 jit_solution(7498013543350280529)
XLA Ops:
  0.6 0.7 fusion.1
  1.3 0.3 convert_reduce_fusion
  1.6 1.4 %convert_reduce_fusion.1 = (s32[]{:T(128)}, s32[512]{0:T(512)S(1)}, s32[512]{0:T(512)S(1)}) fusion(s32[512]{0:T(512)} %param.11, s32[512]{0:T(512)S(1)} %convert_reduce_fusion), kind=kLoop, calls=%fused_computation.22 | loop fusion | flops 13823 | bytes 8196 | tf_op jit(solution)/shard_map/reduce_sum | solution.py:387
  3.0 1.0 select_reduce_fusion
  3.9 0.1 convert_element_type.28
  4.0 0.6 pad.12.refs_1_
  4.6 6.2 %send_rows.1 = f32[5888,128]{1,0:T(8,128)} custom-call(s32[512]{0:T(512)} %get-tuple-element.29.refs_0_.refs_1_, f32[32,128]{1,0:T(8,128)} %pad.12.refs_1_, f32[6144,128]{1,0:T(8,128)} %bitcast.18), custom_call_target="tpu_custom_call" | custom-call | flops 1048576 | bytes 6291456 | tf_op jit(solution)/shard_map/send_rows/pallas_call | solution.py:52
  10.8 7.4 %all-to-all-start = ((f32[32,184,128]{2,1,0:T(8,128)}), f32[32,184,128]{2,1,0:T(8,128)S(1)}, u32[]{:S(2)}, u32[]{:S(2)}) async-start(f32[32,184,128]{2,1,0:T(8,128)} %bitcast.21), calls=%async_computation | async-start | bytes 6029312 | tf_op jit(solution)/shard_map/all_to_all | solution.py:397
  18.2 1.0 fusion.10
  19.2 1.1 fusion.8
  20.3 1.2 fusion.6
  21.4 0.7 pad_maximum_fusion.4
  22.2 1.5 %collective-permute-start.1 = (f32[9,2,2304]{2,1,0:T(2,128)}, f32[9,2,2304]{2,1,0:T(2,128)}, u32[]{:S(2)}, u32[]{:S(2)}) collective-permute-start(f32[9,2,2304]{2,1,0:T(2,128)} %pad_maximum_fusion.4), channel_id=1, source_target_pairs={{8,0},{16,8},{24,16},{0,24},{9,1},{17,9},{25,17},{1,25},{10,2},{18... | collective-permute-start | bytes 497672 | tf_op jit(solution)/shard_map/ppermute | solution.py:365
  23.7 0.7 pad_maximum_fusion.3
  24.4 0.9 copy.11
  25.3 2.0 %fusion.4 = (f32[1,48,2304]{2,1,0:T(8,128)S(1)}, f32[1,48,2304]{2,1,0:T(8,128)}) fusion(f32[5,48,2304]{2,1,0:T(8,128)} %fields_ref), kind=kLoop, calls=%fused_computation.31 | loop fusion | bytes 1769472 | tf_op jit(solution)/shard_map/slice | solution.py:426
  27.2 2.8 %reshape_squeeze.7 = f32[2304,48]{1,0:T(8,128)} reshape(f32[1,48,2304]{2,1,0:T(8,128)} %get-tuple-element.31) | data formatting | bytes 884736 | tf_op jit(solution)/shard_map/reshape;squeeze | solution.py:428
  30.0 1.8 %reshape_squeeze.6 = f32[2304,48]{1,0:T(8,128)} reshape(f32[1,48,2304]{2,1,0:T(8,128)S(1)} %get-tuple-element.30) | data formatting | bytes 884736 | tf_op jit(solution)/shard_map/reshape;squeeze | solution.py:426
  31.7 0.8 and_reduce_fusion
  32.6 0.7 slice_divide_fusion
  33.3 0.8 fusion.9
  34.1 1.0 fusion.7
  35.1 1.1 fusion.5
  36.2 0.1 broadcast_in_dim.63
  36.3 3.3 %pad_maximum_fusion.refs_3_ = f32[2304,128]{1,0:T(8,128)} fusion(f32[2304,16]{1,0:T(8,128)S(1)} %broadcast_in_dim.63, f32[2304,48]{1,0:T(8,128)S(1)} %copy-done.1, f32[2304,48]{1,0:T(8,128)} %reshape_squeeze.6), kind=kLoop, calls=%fused_computation | loop fusion | flops 884736 | bytes 2211840 | tf_op jit(solution)/shard_map/concatenate | solution.py:424
  39.6 0.6 add_select_fusion.1.refs_0_
  40.2 0.7 collective-permute-done.1.high_x
  40.8 0.8 fusion.12
  41.6 0.3 collective-permute-done.low_x
  41.9 0.8 fusion.11
  42.7 0.9 pad_maximum_fusion.1
  43.6 5.0 %collective-permute-start.2 = (f32[9,52,96]{2,1,0:T(8,128)}, f32[9,52,96]{2,1,0:T(8,128)S(1)}, u32[]{:S(2)}, u32[]{:S(2)}) collective-permute-start(f32[9,52,96]{2,1,0:T(8,128)} %get-tuple-element.22), channel_id=1, source_target_pairs={{0,1},{1,2},{2,3},{3,4},{4,5},{5,6},{6,7},{7,0},{8,9},{9,10},{10,1... | collective-permute-start | bytes 539144 | tf_op jit(solution)/shard_map/ppermute | solution.py:364
  48.6 4.7 %collective-permute-start.3 = (f32[9,52,96]{2,1,0:T(8,128)}, f32[9,52,96]{2,1,0:T(8,128)S(1)}, u32[]{:S(2)}, u32[]{:S(2)}) collective-permute-start(f32[9,52,96]{2,1,0:T(8,128)} %get-tuple-element.23), channel_id=1, source_target_pairs={{1,0},{2,1},{3,2},{4,3},{5,4},{6,5},{7,6},{0,7},{9,8},{10,9},{11,1... | collective-permute-start | bytes 539144 | tf_op jit(solution)/shard_map/ppermute | solution.py:365
  53.3 0.8 add_select_fusion.refs_4_
  54.1 15.1 %grow_blocks.1 = (f32[2304,128]{1,0:T(8,128)}, f32[512,128]{1,0:T(8,128)}) custom-call(s32[512]{0:T(512)} %add_select_fusion.1.refs_0_, s32[512]{0:T(512)} %get-tuple-element.29.refs_0_.refs_1_, s32[1]{0:T(128)} %bitcast.6.refs_2_, f32[2304,128]{1,0:T(8,128)} %pad_maximum_fusion.refs_3_, s32[512,128]{1,0:T(8,128)} %add_select_fusion.refs_4_, ...), custom_call_target="tpu_custom_call" | custom-call | flops 16777216 | bytes 8388608 | tf_op jit(solution)/shard_map/grow_blocks/pallas_call | solution.py:166
  69.3 2.5 %reshape.46.cond_ref = f32[48,2304]{1,0:T(8,128)} reshape(f32[2304,48]{1,0:T(8,128)} %bitcast.23) | data formatting | bytes 884736 | tf_op jit(solution)/shard_map/reshape | solution.py:434
  71.7 6.9 %collective-permute-done.2 = f32[9,52,96]{2,1,0:T(8,128)S(1)} collective-permute-done((f32[9,52,96]{2,1,0:T(8,128)}, f32[9,52,96]{2,1,0:T(8,128)S(1)}, u32[]{:S(2)}, u32[]{:S(2)}) %collective-permute-start.2) | collective-permute-done | bytes 179744 | tf_op jit(solution)/shard_map/ppermute | solution.py:364
  78.6 0.8 pad.13.low_y
  79.5 0.7 pad.14.high_y
  80.2 13.5 %advance.1 = f32[5,48,2304]{2,1,0:T(8,128)} custom-call(f32[5,48,2304]{2,1,0:T(8,128)} %fields_ref, f32[3,48,2304]{2,1,0:T(8,128)} %winds_ref, f32[48,2304]{1,0:T(8,128)} %diff_ref, f32[9,2,2304]{2,1,0:T(2,128)} %collective-permute-done.low_x, f32[9,2,2304]{2,1,0:T(2,128)} %collective-permute-done.1.high_x, f32[9,52,128]{2,1,0:T(8,128)} %pad.13.low_y, ...), custom_call_target="tpu_custom_call" | custom-call | flops 67108864 | bytes 16777216 | tf_op jit(solution)/shard_map/advance/pallas_call | solution.py:345
  93.7 0.2 all-to-all-done
  93.8 16.6 %all-to-all-start.1 = ((f32[32,16,128]{2,1,0:T(8,128)}), f32[32,16,128]{2,1,0:T(8,128)S(1)}, u32[]{:S(2)}, u32[]{:S(2)}) async-start(f32[32,16,128]{2,1,0:T(8,128)} %bitcast.9), calls=%async_computation.1 | async-start | bytes 524288 | tf_op jit(solution)/shard_map/all_to_all | solution.py:397
  110.4 0.1 eq.48
  110.5 0.8 select_reduce_fusion.2.refs_0_.source_ref
  111.3 5.6 %place_blocks.1.placed_ref = f32[3072,128]{1,0:T(8,128)} custom-call(s32[256]{0:T(256)} %select_reduce_fusion.2.refs_0_.source_ref, f32[5888,128]{1,0:T(8,128)} %bitcast.20), custom_call_target="tpu_custom_call" | custom-call | flops 1048576 | bytes 5242880 | tf_op jit(solution)/shard_map/place_blocks/pallas_call | solution.py:200
  116.9 4.0 %all-to-all-done.1 = f32[32,16,128]{2,1,0:T(8,128)S(1)} async-done(((f32[32,16,128]{2,1,0:T(8,128)}), f32[32,16,128]{2,1,0:T(8,128)S(1)}, u32[]{:S(2)}, u32[]{:S(2)}) %all-to-all-start.1) | async-done | bytes 262176 | tf_op jit(solution)/shard_map/all_to_all | solution.py:397
  120.8 0.7 copy-done.2
  121.5 2.0 %place_radius.1 = f32[3072,128]{1,0:T(8,128)} custom-call(s32[256]{0:T(256)} %select_reduce_fusion.2.refs_0_.source_ref, f32[512,128]{1,0:T(8,128)} %bitcast.24, f32[3072,128]{1,0:T(8,128)} %place_blocks.1.placed_ref), custom_call_target="tpu_custom_call", output_to_operand_aliasing={{}: (2, {})} | custom-call | flops 65536 | bytes 524288 | tf_op jit(solution)/shard_map/place_radius/pallas_call | solution.py:225
  (14 shorter events, 0.0 us)
Async XLA Ops:
  10.8 83.0 %all-to-all-start = ((f32[32,184,128]{2,1,0:T(8,128)}), f32[32,184,128]{2,1,0:T(8,128)S(1)}, u32[]{:S(2)}, u32[]{:S(2)}) async-start(f32[32,184,128]{2,1,0:T(8,128)} %bitcast.21), calls=%async_computation | async-start | bytes 6029312 | tf_op jit(solution)/shard_map/all_to_all | solution.py:397
  18.2 6.2 %copy-start.3 = (s32[512,128]{1,0:T(8,128)S(1)}, s32[512,128]{1,0:T(8,128)}, u32[]{:S(2)}) copy-start(s32[512,128]{1,0:T(8,128)} %param.10) | copy-start | bytes 786436
  22.2 18.6 %collective-permute-start.1 = (f32[9,2,2304]{2,1,0:T(2,128)}, f32[9,2,2304]{2,1,0:T(2,128)}, u32[]{:S(2)}, u32[]{:S(2)}) collective-permute-start(f32[9,2,2304]{2,1,0:T(2,128)} %pad_maximum_fusion.4), channel_id=1, source_target_pairs={{8,0},{16,8},{24,16},{0,24},{9,1},{17,9},{25,17},{1,25},{10,2},{18... | collective-permute-start | bytes 497672 | tf_op jit(solution)/shard_map/ppermute | solution.py:365
  24.4 17.5 %collective-permute-start = (f32[9,2,2304]{2,1,0:T(2,128)}, f32[9,2,2304]{2,1,0:T(2,128)}, u32[]{:S(2)}, u32[]{:S(2)}) collective-permute-start(f32[9,2,2304]{2,1,0:T(2,128)} %pad_maximum_fusion.3), channel_id=1, source_target_pairs={{0,8},{8,16},{16,24},{24,0},{1,9},{9,17},{17,25},{25,1},{2,10},{10... | collective-permute-start | bytes 497672 | tf_op jit(solution)/shard_map/ppermute | solution.py:364
  31.7 4.6 %copy-start.1 = (f32[2304,48]{1,0:T(8,128)S(1)}, f32[2304,48]{1,0:T(8,128)}, u32[]{:S(2)}) copy-start(f32[2304,48]{1,0:T(8,128)} %reshape_squeeze.7) | copy-start | bytes 1327108
  39.6 13.7 %copy-start.4 = (s32[512,128]{1,0:T(8,128)S(1)}, s32[512,128]{1,0:T(8,128)}, u32[]{:S(2)}) copy-start(s32[512,128]{1,0:T(8,128)} %param.10) | copy-start | bytes 786436
  43.6 35.1 %collective-permute-start.2 = (f32[9,52,96]{2,1,0:T(8,128)}, f32[9,52,96]{2,1,0:T(8,128)S(1)}, u32[]{:S(2)}, u32[]{:S(2)}) collective-permute-start(f32[9,52,96]{2,1,0:T(8,128)} %get-tuple-element.22), channel_id=1, source_target_pairs={{0,1},{1,2},{2,3},{3,4},{4,5},{5,6},{6,7},{7,0},{8,9},{9,10},{10,1... | collective-permute-start | bytes 539144 | tf_op jit(solution)/shard_map/ppermute | solution.py:364
  48.6 30.9 %collective-permute-start.3 = (f32[9,52,96]{2,1,0:T(8,128)}, f32[9,52,96]{2,1,0:T(8,128)S(1)}, u32[]{:S(2)}, u32[]{:S(2)}) collective-permute-start(f32[9,52,96]{2,1,0:T(8,128)} %get-tuple-element.23), channel_id=1, source_target_pairs={{1,0},{2,1},{3,2},{4,3},{5,4},{6,5},{7,6},{0,7},{9,8},{10,9},{11,1... | collective-permute-start | bytes 539144 | tf_op jit(solution)/shard_map/ppermute | solution.py:365
  93.8 17.5 %copy-start = (f32[32,184,128]{2,1,0:T(8,128)}, f32[32,184,128]{2,1,0:T(8,128)S(1)}, u32[]{:S(2)}) copy-start(f32[32,184,128]{2,1,0:T(8,128)S(1)} %all-to-all-done) | copy-start | bytes 9043972
  93.8 27.0 %all-to-all-start.1 = ((f32[32,16,128]{2,1,0:T(8,128)}), f32[32,16,128]{2,1,0:T(8,128)S(1)}, u32[]{:S(2)}, u32[]{:S(2)}) async-start(f32[32,16,128]{2,1,0:T(8,128)} %bitcast.9), calls=%async_computation.1 | async-start | bytes 524288 | tf_op jit(solution)/shard_map/all_to_all | solution.py:397
  120.8 0.7 copy-start.2

commit v3 on v2

--- a/solution.py
+++ b/solution.py
@@ -25,44 +25,74 @@
 
 
 CODE_ROWS = 8
-
-
-def send_kernel(home_cap, send_cap, rows, steps, source_ref, code_ref, drops_ref, out_ref):
+HALF = 6
+
+
+def pack_kernel(f_low, f_high, w_low, w_high, d_low, d_high, low_ref, high_ref):
+    for f, w, d, out in ((f_low, w_low, d_low, low_ref), (f_high, w_high, d_high, high_ref)):
+        out[0:5] = f[...]
+        out[5:8] = w[...]
+        out[8] = d[...]
+
+
+def pack_sides(fields, winds, diffusion):
+    _, width, merged = fields.shape
+    last = merged // LANES - 1
+    specs = []
+    for count in (5, 3):
+        for at in (0, last):
+            specs.append(pl.BlockSpec((count, width, LANES), lambda i, at=at: (0, 0, at)))
+    for at in (0, last):
+        specs.append(pl.BlockSpec((width, LANES), lambda i, at=at: (0, at)))
+    shape = jax.ShapeDtypeStruct((9, width, LANES), jnp.float32)
+    whole = pl.BlockSpec((9, width, LANES), lambda i: (0, 0, 0))
+    return pl.pallas_call(
+        pack_kernel,
+        grid=(1,),
+        out_shape=(shape, shape),
+        in_specs=specs,
+        out_specs=(whole, whole),
+        cost_estimate=cost(1 << 20, 1 << 10),
+        name="pack_sides",
+    )(fields, fields, winds, winds, diffusion, diffusion)
+
+
+def send_kernel(home_cap, send_cap, steps, source_ref, code_ref, drops_ref, out_ref):
     devices = home_cap // send_cap // steps
-    per_device = rows * send_cap + CODE_ROWS
+    per_device = HALF * send_cap + CODE_ROWS
     first = pl.program_id(0) * devices
 
     def body(d, carry):
         start = d * per_device
         for i in range(send_cap):
             b = source_ref[(first + d) * send_cap + i]
-            block = drops_ref[pl.ds(home_cap + b, rows, stride=home_cap), :]
-            out_ref[pl.ds(start + i, rows, stride=send_cap), :] = block
-        out_ref[pl.ds(start + rows * send_cap, 1), :] = code_ref[pl.ds(first + d, 1), :]
+            block = drops_ref[pl.ds(b, HALF, stride=home_cap), :]
+            out_ref[pl.ds(start + i, HALF, stride=send_cap), :] = block
+        out_ref[pl.ds(start + HALF * send_cap, 1), :] = code_ref[pl.ds(first + d, 1), :]
         return carry
 
     lax.fori_loop(0, devices, body, 0)
 
 
 def send_rows(source, codes, planes, home_cap, send_cap):
-    rows = planes.shape[0] // home_cap - 1
     devices = home_cap // send_cap
-    total = devices * (rows * send_cap + CODE_ROWS)
+    total = devices * (HALF * send_cap + CODE_ROWS)
     steps = 4
     return pl.pallas_call(
-        lambda *refs: send_kernel(home_cap, send_cap, rows, steps, *refs),
+        lambda *refs: send_kernel(home_cap, send_cap, steps, *refs),
         grid=(steps,),
         out_shape=jax.ShapeDtypeStruct((total, LANES), jnp.float32),
-        in_specs=[SMEM, VMEM, VMEM],
+        in_specs=[SMEM, VMEM, pl.BlockSpec((HALF * home_cap, LANES), lambda i: (1, 0))],
         out_specs=pl.BlockSpec((total // steps, LANES), lambda i: (i, 0)),
         compiler_params=params(),
-        cost_estimate=cost(6 << 20, 1 << 20),
+        cost_estimate=cost(3 << 20, 1 << 20),
         name="send_rows",
     )(source, codes, planes)
 
 
 def grow_kernel(
     home_cap,
+    send_cap,
     column_ref,
     source_ref,
     live_ref,
@@ -72,7 +102,7 @@
     cond_ref,
     sent_ref,
     picked,
-    radius_out,
+    moved,
     mass,
 ):
     live_count = live_ref[0]
@@ -108,7 +138,13 @@
                 0.04,
             )
         radius = jnp.sqrt(square)
-        radius_out[rows, :] = radius
+        moved[rows, :] = radius
+        moved[pl.ds(home_cap + at, BATCH), :] = solute
+        moved[pl.ds(2 * home_cap + at, BATCH), :] = weight
+        for r in range(3, 6):
+            spot = drops_ref[pl.ds(r * home_cap + at, BATCH), :]
+            speed = drops_ref[pl.ds((r + 3) * home_cap + at, BATCH), :]
+            moved[pl.ds(r * home_cap + at, BATCH), :] = spot + 0.1 * speed
         grown = weight * (radius * square - start * start * start)
         block = at + lax.broadcasted_iota(jnp.int32, (BATCH, LANES), 0)
         mass[rows, :] = jnp.where(block < live_count, grown, 0.0)
@@ -119,7 +155,9 @@
     def send(g, carry):
         for i in range(8):
             b = g * 8 + i
-            sent_ref[pl.ds(b, 1), :] = radius_out[pl.ds(source_ref[b], 1), :]
+            start = (b // send_cap) * (HALF * send_cap) + b % send_cap
+            block = moved[pl.ds(source_ref[b], HALF, stride=home_cap), :]
+            sent_ref[pl.ds(start, HALF, stride=send_cap), :] = block
         return carry
 
     lax.fori_loop(0, home_cap // 8, send, 0)
@@ -160,79 +198,58 @@
     lax.fori_loop(0, home_cap // 8, scatter, 0)
 
 
-def grow_blocks(column, source, live_count, table, level, planes):
+def grow_blocks(column, source, live_count, table, level, planes, send_cap):
     home_cap = level.shape[0]
     scratch = pltpu.VMEM((home_cap, LANES), jnp.float32)
     return pl.pallas_call(
-        lambda *refs: grow_kernel(home_cap, *refs),
+        lambda *refs: grow_kernel(home_cap, send_cap, *refs),
         out_shape=(
             jax.ShapeDtypeStruct(table.shape, jnp.float32),
-            jax.ShapeDtypeStruct((home_cap, LANES), jnp.float32),
+            jax.ShapeDtypeStruct((HALF * home_cap, LANES), jnp.float32),
         ),
         in_specs=[SMEM, SMEM, SMEM, VMEM, VMEM, VMEM],
         out_specs=(VMEM, VMEM),
-        scratch_shapes=[scratch, scratch, scratch],
+        scratch_shapes=[scratch, pltpu.VMEM((HALF * home_cap, LANES), jnp.float32), scratch],
         compiler_params=params(),
         cost_estimate=cost(8 << 20, 1 << 24),
         name="grow_blocks",
     )(column, source, live_count, table, level, planes)
 
 
-def place_kernel(home_cap, send_cap, rows, source_ref, arrived_ref, out_ref):
-    per_device = rows * send_cap + CODE_ROWS
+def place_kernel(per_device, send_cap, source_ref, arrived_ref, *refs):
+    out_ref = refs[-1]
 
     def body(g, carry):
         for i in range(8):
             j = g * 8 + i
             source = source_ref[j]
             first = (source // send_cap) * per_device + source % send_cap
-            block = arrived_ref[pl.ds(first, rows, stride=send_cap), :]
-            out_ref[pl.ds(OWN_BLK + j, rows, stride=OWN_BLK), :] = block
+            block = arrived_ref[pl.ds(first, HALF, stride=send_cap), :]
+            out_ref[pl.ds(j, HALF, stride=OWN_BLK), :] = block
         return carry
 
     lax.fori_loop(0, OWN_BLK // 8, body, 0)
-    for r in range(3, 6):
-        at = pl.ds(r * OWN_BLK, OWN_BLK)
-        out_ref[at, :] = out_ref[at, :] + 0.1 * out_ref[pl.ds((r + 3) * OWN_BLK, OWN_BLK), :]
-
-
-def place_blocks(source, arrived, home_cap, send_cap, rows):
+
+
+def place_half(source, arrived, devices, send_cap, half, into):
+    arrays = [source, arrived]
+    specs = [SMEM, VMEM]
+    aliases = {}
+    if into is not None:
+        arrays.append(into)
+        specs.append(pl.BlockSpec(memory_space=pl.ANY))
+        aliases = {2: 0}
     return pl.pallas_call(
-        lambda *refs: place_kernel(home_cap, send_cap, rows, *refs),
-        out_shape=jax.ShapeDtypeStruct(((rows + 1) * OWN_BLK, LANES), jnp.float32),
-        in_specs=[SMEM, VMEM],
-        out_specs=VMEM,
+        lambda *refs: place_kernel(arrived.shape[0] // devices, send_cap, *refs),
+        grid=(1,),
+        out_shape=jax.ShapeDtypeStruct((2 * HALF * OWN_BLK, LANES), jnp.float32),
+        in_specs=specs,
+        out_specs=pl.BlockSpec((HALF * OWN_BLK, LANES), lambda i: (half, 0)),
+        input_output_aliases=aliases,
         compiler_params=params(),
-        cost_estimate=cost(5 << 20, 1 << 20),
-        name="place_blocks",
-    )(source, arrived)
-
-
-def place_radius_kernel(source_ref, radius_ref, placed_ref, out_ref, rows_ref, sem):
-    def body(g, carry):
-        for i in range(8):
-            j = g * 8 + i
-            rows_ref[pl.ds(j, 1), :] = radius_ref[pl.ds(source_ref[j], 1), :]
-        return carry
-
-    lax.fori_loop(0, OWN_BLK // 8, body, 0)
-    copy = pltpu.make_async_copy(rows_ref, out_ref.at[pl.ds(0, OWN_BLK), :], sem)
-    copy.start()
-    copy.wait()
-
-
-def place_radius(source, radius, placed):
-    return pl.pallas_call(
-        place_radius_kernel,
-        out_shape=jax.ShapeDtypeStruct(placed.shape, jnp.float32),
-        in_specs=[SMEM, VMEM, pl.BlockSpec(memory_space=pl.ANY)],
-        out_specs=pl.BlockSpec(memory_space=pl.ANY),
-        scratch_shapes=[pltpu.VMEM((OWN_BLK, LANES), jnp.float32), pltpu.SemaphoreType.DMA],
-        input_output_aliases={2: 0},
-        compiler_params=params(),
-        cost_estimate=cost(1 << 19, 1 << 16),
-        name="place_radius",
-    )(source, radius, placed)
+        cost_estimate=cost(3 << 20, 1 << 20),
+        name="place_half",
+    )(*arrays)
 
 
 def stencil_kernel(
@@ -262,10 +279,10 @@
         else:
             own = diff_ref[...]
         ext[k, inner, core] = own
-        ext[k, ROW0 - 2 : ROW0, core] = low_x[k]
-        ext[k, ROW0 + width : ROW0 + width + 2, core] = high_x[k]
-        ext[k, ROW0 - 2 : ROW0 + width + 2, 0:LANES] = low_y[k]
-        ext[k, ROW0 - 2 : ROW0 + width + 2, LANES + merged : lanes] = high_y[k]
+        ext[k, ROW0 - 2 : ROW0, :] = low_x[k]
+        ext[k, ROW0 + width : ROW0 + width + 2, :] = high_x[k]
+        ext[k, inner, 0:LANES] = low_y[k]
+        ext[k, inner, LANES + merged : lanes] = high_y[k]
 
     chunks = range(ROW0 - 8, ROW0 + width + 8, 8)
     z = (lax.broadcasted_iota(jnp.int32, (8, lanes), 1) + (NZ - LANES % NZ)) % NZ
@@ -375,8 +392,9 @@
     rows = droplets.shape[1] - 1
     column_count = width * merged // NZ
 
-    every = slice(None)
-    strip = 2 * NZ
+    sides = pack_sides(fields, winds, diffusion)
+    sides, balance_list = lax.optimization_barrier((sides, balance_list))
+    low_y, high_y = both_ways(*sides, "gy")
     live = balance_list >= 0
     owner = jnp.where(live, balance_list // OWN_BLK, devices)
     slot = balance_list % OWN_BLK
@@ -397,27 +415,20 @@
         return lax.all_to_all(x, everyone, split_axis=0, concat_axis=0, tiled=True)
 
     outgoing = send_rows(send_source, codes, planes, home_cap, send_cap)
-    outgoing, fields, winds, diffusion, cells = lax.optimization_barrier(
-        (outgoing, fields, winds, diffusion, cells)
+    outgoing, low_y, high_y, fields, winds, diffusion, cells = lax.optimization_barrier(
+        (outgoing, low_y, high_y, fields, winds, diffusion, cells)
     )
     arrived = exchange(outgoing)
 
-    def edge(xs, ys):
+    def edge(xs):
         grids = (fields, winds, diffusion[None])
-        return jnp.concatenate([g[:, xs, ys] for g in grids], axis=0)
-
-    low_x, high_x = both_ways(
-        edge(slice(0, 2), every), edge(slice(width - 2, width), every), "gx"
-    )
-
-    def side(ys):
-        return jnp.concatenate([low_x[:, :, ys], edge(every, ys), high_x[:, :, ys]], axis=1)
-
-    sides = (side(slice(0, strip)), side(slice(merged - strip, merged)))
-    sides, column = lax.optimization_barrier((sides, cells[:, 0] // NZ))
-    low_y, high_y = both_ways(*sides, "gy")
-    low_y = jnp.pad(low_y, ((0, 0), (0, 0), (LANES - strip, 0)))
-    high_y = jnp.pad(high_y, ((0, 0), (0, 0), (0, LANES - strip)))
+        own = jnp.concatenate([g[:, xs] for g in grids], axis=0)
+        return jnp.concatenate([low_y[:, xs], own, high_y[:, xs]], axis=2)
+
+    x_edges = (edge(slice(0, 2)), edge(slice(width - 2, width)))
+    x_edges, cells, fields = lax.optimization_barrier((x_edges, cells, fields))
+    column = cells[:, 0] // NZ
+    low_x, high_x = both_ways(*x_edges, "gx")
 
     level = cells % NZ
     gap = jnp.zeros((column_count, LANES // 2 - NZ), jnp.float32)
@@ -430,23 +441,27 @@
         ],
         axis=1,
     )
-    condensed, radius = grow_blocks(column, send_source, live_count, table, level, planes)
+    condensed, second = grow_blocks(
+        column, send_source, live_count, table, level, planes, send_cap
+    )
+    second, low_x, high_x = lax.optimization_barrier((second, low_x, high_x))
+    arrived, low_x, high_x = lax.optimization_barrier((arrived, low_x, high_x))
+    arrived_second = exchange(second)
     condensed = condensed[:, :NZ].reshape(width, merged)
     fields_out = advance(fields, winds, diffusion, low_x, high_x, low_y, high_y, condensed)
 
-    arrived, radius, fields_out = lax.optimization_barrier((arrived, radius, fields_out))
-    arrived_radius = exchange(radius)
     per_device_rows = arrived.shape[0] // devices
     arrived_codes = arrived.reshape(devices, per_device_rows, LANES)[
-        :, rows * send_cap, :send_cap
+        :, HALF * send_cap, :send_cap
     ].reshape(-1)
     own = lax.iota(jnp.int32, OWN_BLK).astype(jnp.float32)
     source = jnp.sum(
         jnp.where(arrived_codes[None, :] == own[:, None], order[None, :], 0), axis=1
     )
-    placed = place_blocks(source, arrived, home_cap, send_cap, rows)
-    placed = place_radius(source, arrived_radius, placed)
-    droplets_out = placed.reshape(rows + 1, OWN_BLK, LANES).transpose(1, 0, 2)
+    placed = place_half(source, arrived, devices, send_cap, 1, None)
+    placed, fields_out = lax.optimization_barrier((placed, fields_out))
+    placed = place_half(source, arrived_second, devices, send_cap, 0, placed)
+    droplets_out = placed.reshape(2 * HALF, OWN_BLK, LANES).transpose(1, 0, 2)
     return (fields_out, droplets_out)
 
 

time: 124 us -> 113 us (0.911)
  starting transfers between devices: 35.1 us -> 15.2 us
  waiting for transfers between devices: 12 us -> 25.7 us
  Pallas kernels: 42.3 us -> 47.5 us
  local copies, waits for them, and re-layouts: 20.6 us -> 15.7 us
  other arithmetic: 12.7 us -> 7.97 us
    all_to_all x2, waiting for transfers between devices: 4.13 us -> 24 us  [exchange(): return lax.all_to_all(x, everyone, split_axis=0, concat_axis=0, tiled=True)]
    all_to_all x2, starting transfers between devices: 23.9 us -> 7.39 us  [exchange(): return lax.all_to_all(x, everyone, split_axis=0, concat_axis=0, tiled=True)]
    ppermute x2, waiting for transfers between devices: 7.17 us -> 0.01 us  [both_ways(): lax.ppermute(high_edge, axis, [(i, (i + 1) % count) for i in range(count)])]
    pallas_call x4 -> x5, Pallas kernels: 28.9 us -> 34.1 us  [the longest x1 18.9 us: grow_blocks(): pl.pallas_call(lambda *refs: grow_kernel(home_cap, send_cap, *refs), out_...]
    slice x8 -> x4, local copies, waits for them, and re-layouts: 7.7 us -> 3.28 us  [the longest x3 3.27 us: edge(): own = jnp.concatenate([g[:, xs] for g in grids], axis=0)]
    unnamed x10 -> x16, local copies, waits for them, and re-layouts: 0.71 us -> 2.51 us
    ppermute x2, starting transfers between devices: 6.23 us -> 4.54 us  [both_ways(): lax.ppermute(low_edge, axis, [((i + 1) % count, i) for i in range(count)])]
    ppermute x2, starting transfers between devices: 4.98 us -> 3.3 us  [both_ways(): lax.ppermute(high_edge, axis, [(i, (i + 1) % count) for i in range(count)])]
  transfers between devices with their start and end apart: 6 -> 6, of which waited for: 5 -> 3; matrix products, arithmetic and copies ran while one was open for 23% -> 17% of each run, Pallas kernels for 28% -> 37%
where the time goes in v3:
time: 113 us
  Pallas kernels  47.5 us (42%)
  waiting for transfers between devices  25.7 us (23%)
  local copies, waits for them, and re-layouts  15.7 us (14%)
  starting transfers between devices  15.2 us (13%)
  other arithmetic  7.97 us (7%)
    all_to_all x2, waiting for transfers between devices, exchange(): return lax.all_to_all(x, everyone, split_axis=0, concat_axis=0, tiled=True)  24 us
    pallas_call x1, Pallas kernels, grow_blocks(): pl.pallas_call(lambda *refs: grow_kernel(home_cap, send_cap, *refs), out_...  18.9 us
    pallas_call x1, Pallas kernels, advance(): pl.pallas_call(stencil_kernel, out_shape=jax.ShapeDtypeStruct(fields.shap...  13.4 us
    pallas_call x2, Pallas kernels, place_half(): pl.pallas_call(lambda *refs: place_kernel(arrived.shape[0] // devices, se...  8.85 us
    all_to_all x2, starting transfers between devices, exchange(): return lax.all_to_all(x, everyone, split_axis=0, concat_axis=0, tiled=True)  7.39 us
    ppermute x2, starting transfers between devices, both_ways(): lax.ppermute(low_edge, axis, [((i + 1) % count, i) for i in range(count)])  4.54 us
    pallas_call x1, Pallas kernels, send_rows(): pl.pallas_call(lambda *refs: send_kernel(home_cap, send_cap, steps, *refs...  4.46 us
    ppermute x2, starting transfers between devices, both_ways(): lax.ppermute(high_edge, axis, [(i, (i + 1) % count) for i in range(count)])  3.3 us
  transfers between devices with their start and end apart: 6, of which 3 were waited for; matrix products, arithmetic and copies ran while one was open for 17% of the time, Pallas kernels for 37%

profile of v3, /device:TPU:0, one launch (start us, length us, event | category | flops | bytes accessed | tf_op | source)
XLA Modules:
  0.0 112.8 jit_solution(4729039408006461479)
XLA Ops:
  0.6 0.0 copy-start.7
  0.6 1.8 %pack_sides.1 = (f32[9,48,128]{2,1,0:T(8,128)}, f32[9,48,128]{2,1,0:T(8,128)}) custom-call(f32[5,48,2304]{2,1,0:T(8,128)} %fields_ref, f32[5,48,2304]{2,1,0:T(8,128)} %fields_ref, f32[3,48,2304]{2,1,0:T(8,128)} %winds_ref, f32[3,48,2304]{2,1,0:T(8,128)} %winds_ref, f32[48,2304]{1,0:T(8,128)} %diff_ref, f32[48,2304]{1,0:T(8,128)} %diff_ref), custom_call_target="tpu_custom_call" | custom-call | flops 1024 | bytes 1048576 | tf_op jit(solution)/shard_map/pack_sides/pallas_call | solution.py:49
  2.5 3.0 %collective-permute-start = (f32[9,48,128]{2,1,0:T(8,128)}, f32[9,48,128]{2,1,0:T(8,128)S(1)}, u32[]{:S(2)}, u32[]{:S(2)}) collective-permute-start(f32[9,48,128]{2,1,0:T(8,128)} %get-tuple-element.31), channel_id=1, source_target_pairs={{0,1},{1,2},{2,3},{3,4},{4,5},{5,6},{6,7},{7,0},{8,9},{9,10},{10,1... | collective-permute-start | bytes 663560 | tf_op jit(solution)/shard_map/ppermute | solution.py:381
  5.5 3.0 %collective-permute-start.1 = (f32[9,48,128]{2,1,0:T(8,128)}, f32[9,48,128]{2,1,0:T(8,128)S(1)}, u32[]{:S(2)}, u32[]{:S(2)}) collective-permute-start(f32[9,48,128]{2,1,0:T(8,128)} %get-tuple-element.32), channel_id=1, source_target_pairs={{1,0},{2,1},{3,2},{4,3},{5,4},{6,5},{7,6},{0,7},{9,8},{10,9},{11,1... | collective-permute-start | bytes 663560 | tf_op jit(solution)/shard_map/ppermute | solution.py:382
  8.5 0.0 copy-done.7
  8.5 0.7 convert_reduce_fusion.1
  9.2 0.2 convert_reduce_fusion
  9.5 0.9 select_reduce_fusion
  10.5 0.1 convert_element_type.24
  10.5 0.6 pad.4.refs_1_
  11.1 4.5 %send_rows.1 = f32[3328,128]{1,0:T(8,128)} custom-call(s32[512]{0:T(512)} %get-tuple-element.55.refs_0_.refs_1_, f32[32,128]{1,0:T(8,128)} %pad.4.refs_1_, f32[6144,128]{1,0:T(8,128)} %bitcast.18), custom_call_target="tpu_custom_call" | custom-call | flops 1048576 | bytes 3145728 | tf_op jit(solution)/shard_map/send_rows/pallas_call | solution.py:81
  15.6 0.0 collective-permute-done.low_y
  15.6 1.7 %collective-permute-done.1.high_y = f32[9,48,128]{2,1,0:T(8,128)S(1)} collective-permute-done((f32[9,48,128]{2,1,0:T(8,128)}, f32[9,48,128]{2,1,0:T(8,128)S(1)}, u32[]{:S(2)}, u32[]{:S(2)}) %collective-permute-start.1) | collective-permute-done | bytes 221216 | tf_op jit(solution)/shard_map/ppermute | solution.py:382
  17.3 1.2 %fusion.6 = (f32[3,2,2304]{2,1,0:T(2,128)S(1)}, f32[3,2,2304]{2,1,0:T(2,128)S(1)}) fusion(f32[3,48,2304]{2,1,0:T(8,128)} %winds_ref), kind=kLoop, calls=%fused_computation.31 | loop fusion | bytes 221184 | tf_op jit(solution)/shard_map/slice | solution.py:425
  18.5 0.9 fusion.7
  19.4 4.7 %all-to-all-start = ((f32[32,104,128]{2,1,0:T(8,128)}), f32[32,104,128]{2,1,0:T(8,128)S(1)}, u32[]{:S(2)}, u32[]{:S(2)}) async-start(f32[32,104,128]{2,1,0:T(8,128)} %bitcast.21), calls=%async_computation | async-start | bytes 3407872 | tf_op jit(solution)/shard_map/all_to_all | solution.py:415
  24.1 0.0 copy-done.3
  24.1 0.0 copy-done.4
  24.2 1.2 %fusion.5 = (f32[5,2,2304]{2,1,0:T(2,128)S(1)}, f32[5,2,2304]{2,1,0:T(2,128)S(1)}) fusion(f32[5,48,2304]{2,1,0:T(8,128)} %fields_ref), kind=kLoop, calls=%fused_computation.30 | loop fusion | bytes 368640 | tf_op jit(solution)/shard_map/slice | solution.py:425
  25.3 0.1 pad_maximum_fusion.2
  25.4 0.8 pad_maximum_fusion.1
  26.2 2.0 %fusion.4 = (f32[1,48,2304]{2,1,0:T(8,128)}, f32[1,48,2304]{2,1,0:T(8,128)S(1)}) fusion(f32[5,48,2304]{2,1,0:T(8,128)} %fields_ref), kind=kLoop, calls=%fused_computation.29 | loop fusion | bytes 1769472 | tf_op jit(solution)/shard_map/slice | solution.py:437
  28.2 1.7 %reshape_squeeze.6 = f32[2304,48]{1,0:T(8,128)S(1)} reshape(f32[1,48,2304]{2,1,0:T(8,128)} %get-tuple-element.56) | data formatting | bytes 884736 | tf_op jit(solution)/shard_map/reshape;squeeze | solution.py:437
  29.9 1.8 %reshape_squeeze.7 = f32[2304,48]{1,0:T(8,128)} reshape(f32[1,48,2304]{2,1,0:T(8,128)S(1)} %get-tuple-element.57) | data formatting | bytes 884736 | tf_op jit(solution)/shard_map/reshape;squeeze | solution.py:439
  31.7 1.1 copy.11
  32.7 0.0 copy-start.2
  32.8 0.3 collective-permute-start.2
  33.1 1.5 %collective-permute-start.3 = (f32[9,2,2560]{2,1,0:T(2,128)}, f32[9,2,2560]{2,1,0:T(2,128)S(1)}, u32[]{:S(2)}, u32[]{:S(2)}) collective-permute-start(f32[9,2,2560]{2,1,0:T(2,128)} %pad_maximum_fusion.1), channel_id=1, source_target_pairs={{8,0},{16,8},{24,16},{0,24},{9,1},{17,9},{25,17},{1,25},{10,2},{18... | collective-permute-start | bytes 552968 | tf_op jit(solution)/shard_map/ppermute | solution.py:382
  34.6 1.8 %add_select_fusion.refs_4_ = s32[512,128]{1,0:T(8,128)} fusion(s32[512,128]{1,0:T(8,128)} %param.10), kind=kLoop, calls=%fused_computation.8 | loop fusion | flops 393216 | bytes 524288 | tf_op jit(solution)/shard_map/jit(remainder)/select_n | solution.py:433
  36.4 0.1 broadcast_in_dim.61
  36.5 0.0 copy-done.2
  36.5 2.0 %pad_maximum_fusion.refs_3_ = f32[2304,128]{1,0:T(8,128)} fusion(f32[2304,16]{1,0:T(8,128)S(1)} %broadcast_in_dim.61, f32[2304,48]{1,0:T(8,128)S(1)} %copy-done.2, f32[2304,48]{1,0:T(8,128)S(1)} %reshape_squeeze.6), kind=kLoop, calls=%fused_computation | loop fusion | flops 884736 | bytes 2211840 | tf_op jit(solution)/shard_map/concatenate | solution.py:435
  38.5 0.6 add_select_fusion.1.refs_0_
  39.1 18.9 %grow_blocks.1 = (f32[2304,128]{1,0:T(8,128)}, f32[3072,128]{1,0:T(8,128)}) custom-call(s32[512]{0:T(512)} %add_select_fusion.1.refs_0_, s32[512]{0:T(512)} %get-tuple-element.55.refs_0_.refs_1_, s32[1]{0:T(128)} %bitcast.6.refs_2_, f32[2304,128]{1,0:T(8,128)} %pad_maximum_fusion.refs_3_, s32[512,128]{1,0:T(8,128)} %add_select_fusion.refs_4_, ...), custom_call_target="tpu_custom_call" | custom-call | flops 16777216 | bytes 8388608 | tf_op jit(solution)/shard_map/grow_blocks/pallas_call | solution.py:204
  58.0 0.0 collective-permute-done.2.low_x
  58.0 0.0 collective-permute-done.3.high_x
  58.0 0.7 copy-done.5
  58.7 0.7 copy-done.6
  59.3 6.4 %all-to-all-done = f32[32,104,128]{2,1,0:T(8,128)S(1)} async-done(((f32[32,104,128]{2,1,0:T(8,128)}), f32[32,104,128]{2,1,0:T(8,128)S(1)}, u32[]{:S(2)}, u32[]{:S(2)}) %all-to-all-start) | async-done | bytes 1703968 | tf_op jit(solution)/shard_map/all_to_all | solution.py:415
  65.8 2.7 %all-to-all-start.1 = ((f32[32,96,128]{2,1,0:T(8,128)}), f32[32,96,128]{2,1,0:T(8,128)S(1)}, u32[]{:S(2)}, u32[]{:S(2)}) async-start(f32[32,96,128]{2,1,0:T(8,128)} %bitcast.25), calls=%async_computation.1 | async-start | bytes 3145728 | tf_op jit(solution)/shard_map/all_to_all | solution.py:415
  68.5 2.5 %reshape.47.cond_ref = f32[48,2304]{1,0:T(8,128)} reshape(f32[2304,48]{1,0:T(8,128)} %bitcast.26) | data formatting | bytes 884736 | tf_op jit(solution)/shard_map/reshape | solution.py:450
  71.0 0.1 eq.48
  71.1 0.8 select_reduce_fusion.2.refs_0_
  71.8 4.4 %place_half.2.refs_2_ = f32[3072,128]{1,0:T(8,128)} custom-call(s32[256]{0:T(256)} %select_reduce_fusion.2.refs_0_, f32[3328,128]{1,0:T(8,128)} %bitcast.20), custom_call_target="tpu_custom_call" | custom-call | flops 1048576 | bytes 3145728 | tf_op jit(solution)/shard_map/place_half/pallas_call | solution.py:242
  76.3 13.4 %advance.1 = f32[5,48,2304]{2,1,0:T(8,128)} custom-call(f32[5,48,2304]{2,1,0:T(8,128)} %fields_ref, f32[3,48,2304]{2,1,0:T(8,128)} %winds_ref, f32[48,2304]{1,0:T(8,128)} %diff_ref, f32[9,2,2560]{2,1,0:T(2,128)} %copy-done.5, f32[9,2,2560]{2,1,0:T(2,128)} %copy-done.6, f32[9,48,128]{2,1,0:T(8,128)} %copy-done.3, f32[9,48,128]{2,1,0:T(8,128)} %copy-done.4, ...), custom_call_target="tpu_custom_call" | custom-call | flops 67108864 | bytes 16777216 | tf_op jit(solution)/shard_map/advance/pallas_call | solution.py:362
  89.7 17.6 %all-to-all-done.1 = f32[32,96,128]{2,1,0:T(8,128)S(1)} async-done(((f32[32,96,128]{2,1,0:T(8,128)}), f32[32,96,128]{2,1,0:T(8,128)S(1)}, u32[]{:S(2)}, u32[]{:S(2)}) %all-to-all-start.1) | async-done | bytes 1572896 | tf_op jit(solution)/shard_map/all_to_all | solution.py:415
  107.3 1.1 %copy-done.1 = f32[32,96,128]{2,1,0:T(8,128)} copy-done((f32[32,96,128]{2,1,0:T(8,128)}, f32[32,96,128]{2,1,0:T(8,128)S(1)}, u32[]{:S(2)}) %copy-start.1) | copy-done | bytes 1572888
  108.4 4.4 %place_half.3 = f32[3072,128]{1,0:T(8,128)} custom-call(s32[256]{0:T(256)} %select_reduce_fusion.2.refs_0_, f32[3072,128]{1,0:T(8,128)} %bitcast.22, f32[3072,128]{1,0:T(8,128)} %place_half.2.refs_2_), custom_call_target="tpu_custom_call", output_to_operand_aliasing={{}: (2, {})} | custom-call | flops 1048576 | bytes 3145728 | tf_op jit(solution)/shard_map/place_half/pallas_call | solution.py:242
  (14 shorter events, 0.1 us)
Async XLA Ops:
  0.6 7.9 %copy-start.7 = (s32[512]{0:T(512)S(1)}, s32[512]{0:T(512)}, u32[]{:S(2)}) copy-start(s32[512]{0:T(512)} %param.11) | copy-start | bytes 6148
  2.5 13.1 %collective-permute-start = (f32[9,48,128]{2,1,0:T(8,128)}, f32[9,48,128]{2,1,0:T(8,128)S(1)}, u32[]{:S(2)}, u32[]{:S(2)}) collective-permute-start(f32[9,48,128]{2,1,0:T(8,128)} %get-tuple-element.31), channel_id=1, source_target_pairs={{0,1},{1,2},{2,3},{3,4},{4,5},{5,6},{6,7},{7,0},{8,9},{9,10},{10,1... | collective-permute-start | bytes 663560 | tf_op jit(solution)/shard_map/ppermute | solution.py:381
  5.5 11.8 %collective-permute-start.1 = (f32[9,48,128]{2,1,0:T(8,128)}, f32[9,48,128]{2,1,0:T(8,128)S(1)}, u32[]{:S(2)}, u32[]{:S(2)}) collective-permute-start(f32[9,48,128]{2,1,0:T(8,128)} %get-tuple-element.32), channel_id=1, source_target_pairs={{1,0},{2,1},{3,2},{4,3},{5,4},{6,5},{7,6},{0,7},{9,8},{10,9},{11,1... | collective-permute-start | bytes 663560 | tf_op jit(solution)/shard_map/ppermute | solution.py:382
  15.6 8.5 %copy-start.3 = (f32[9,48,128]{2,1,0:T(8,128)}, f32[9,48,128]{2,1,0:T(8,128)S(1)}, u32[]{:S(2)}) copy-start(f32[9,48,128]{2,1,0:T(8,128)S(1)} %collective-permute-done.low_y) | copy-start | bytes 663556
  17.3 6.8 %copy-start.4 = (f32[9,48,128]{2,1,0:T(8,128)}, f32[9,48,128]{2,1,0:T(8,128)S(1)}, u32[]{:S(2)}) copy-start(f32[9,48,128]{2,1,0:T(8,128)S(1)} %collective-permute-done.1.high_y) | copy-start | bytes 663556
  19.4 46.3 %all-to-all-start = ((f32[32,104,128]{2,1,0:T(8,128)}), f32[32,104,128]{2,1,0:T(8,128)S(1)}, u32[]{:S(2)}, u32[]{:S(2)}) async-start(f32[32,104,128]{2,1,0:T(8,128)} %bitcast.21), calls=%async_computation | async-start | bytes 3407872 | tf_op jit(solution)/shard_map/all_to_all | solution.py:415
  32.7 3.7 %copy-start.2 = (f32[2304,48]{1,0:T(8,128)S(1)}, f32[2304,48]{1,0:T(8,128)}, u32[]{:S(2)}) copy-start(f32[2304,48]{1,0:T(8,128)} %reshape_squeeze.7) | copy-start | bytes 1327108
  32.8 25.2 %collective-permute-start.2 = (f32[9,2,2560]{2,1,0:T(2,128)S(1)}, f32[9,2,2560]{2,1,0:T(2,128)S(1)}, u32[]{:S(2)}, u32[]{:S(2)}) collective-permute-start(f32[9,2,2560]{2,1,0:T(2,128)S(1)} %pad_maximum_fusion.2), channel_id=1, source_target_pairs={{0,8},{8,16},{16,24},{24,0},{1,9},{9,17},{17,25},{25,1},{2,10},{10... | collective-permute-start | bytes 552968 | tf_op jit(solution)/shard_map/ppermute | solution.py:381
  33.1 24.9 %collective-permute-start.3 = (f32[9,2,2560]{2,1,0:T(2,128)}, f32[9,2,2560]{2,1,0:T(2,128)S(1)}, u32[]{:S(2)}, u32[]{:S(2)}) collective-permute-start(f32[9,2,2560]{2,1,0:T(2,128)} %pad_maximum_fusion.1), channel_id=1, source_target_pairs={{8,0},{16,8},{24,16},{0,24},{9,1},{17,9},{25,17},{1,25},{10,2},{18... | collective-permute-start | bytes 552968 | tf_op jit(solution)/shard_map/ppermute | solution.py:382
  58.0 0.7 copy-start.5
  58.7 0.7 copy-start.6
  65.8 5.2 %copy-start = (f32[32,104,128]{2,1,0:T(8,128)}, f32[32,104,128]{2,1,0:T(8,128)S(1)}, u32[]{:S(2)}) copy-start(f32[32,104,128]{2,1,0:T(8,128)S(1)} %all-to-all-done) | copy-start | bytes 5111812
  65.8 41.5 %all-to-all-start.1 = ((f32[32,96,128]{2,1,0:T(8,128)}), f32[32,96,128]{2,1,0:T(8,128)S(1)}, u32[]{:S(2)}, u32[]{:S(2)}) async-start(f32[32,96,128]{2,1,0:T(8,128)} %bitcast.25), calls=%async_computation.1 | async-start | bytes 3145728 | tf_op jit(solution)/shard_map/all_to_all | solution.py:415
  107.3 1.1 %copy-start.1 = (f32[32,96,128]{2,1,0:T(8,128)}, f32[32,96,128]{2,1,0:T(8,128)S(1)}, u32[]{:S(2)}) copy-start(f32[32,96,128]{2,1,0:T(8,128)S(1)} %all-to-all-done.1) | copy-start | bytes 4718596

commit v4 on v2

--- a/solution.py
+++ b/solution.py
@@ -25,6 +25,35 @@
 
 
 CODE_ROWS = 8
+
+
+def pack_kernel(f_low, f_high, w_low, w_high, d_low, d_high, low_ref, high_ref):
+    for f, w, d, out in ((f_low, w_low, d_low, low_ref), (f_high, w_high, d_high, high_ref)):
+        out[0:5] = f[...]
+        out[5:8] = w[...]
+        out[8] = d[...]
+
+
+def pack_sides(fields, winds, diffusion):
+    _, width, merged = fields.shape
+    last = merged // LANES - 1
+    specs = []
+    for count in (5, 3):
+        for at in (0, last):
+            specs.append(pl.BlockSpec((count, width, LANES), lambda i, at=at: (0, 0, at)))
+    for at in (0, last):
+        specs.append(pl.BlockSpec((width, LANES), lambda i, at=at: (0, at)))
+    shape = jax.ShapeDtypeStruct((9, width, LANES), jnp.float32)
+    whole = pl.BlockSpec((9, width, LANES), lambda i: (0, 0, 0))
+    return pl.pallas_call(
+        pack_kernel,
+        grid=(1,),
+        out_shape=(shape, shape),
+        in_specs=specs,
+        out_specs=(whole, whole),
+        cost_estimate=cost(1 << 20, 1 << 10),
+        name="pack_sides",
+    )(fields, fields, winds, winds, diffusion, diffusion)
 
 
 def send_kernel(home_cap, send_cap, rows, steps, source_ref, code_ref, drops_ref, out_ref):
@@ -262,10 +291,10 @@
         else:
             own = diff_ref[...]
         ext[k, inner, core] = own
-        ext[k, ROW0 - 2 : ROW0, core] = low_x[k]
-        ext[k, ROW0 + width : ROW0 + width + 2, core] = high_x[k]
-        ext[k, ROW0 - 2 : ROW0 + width + 2, 0:LANES] = low_y[k]
-        ext[k, ROW0 - 2 : ROW0 + width + 2, LANES + merged : lanes] = high_y[k]
+        ext[k, ROW0 - 2 : ROW0, :] = low_x[k]
+        ext[k, ROW0 + width : ROW0 + width + 2, :] = high_x[k]
+        ext[k, inner, 0:LANES] = low_y[k]
+        ext[k, inner, LANES + merged : lanes] = high_y[k]
 
     chunks = range(ROW0 - 8, ROW0 + width + 8, 8)
     z = (lax.broadcasted_iota(jnp.int32, (8, lanes), 1) + (NZ - LANES % NZ)) % NZ
@@ -375,8 +404,9 @@
     rows = droplets.shape[1] - 1
     column_count = width * merged // NZ
 
-    every = slice(None)
-    strip = 2 * NZ
+    sides = pack_sides(fields, winds, diffusion)
+    sides, balance_list = lax.optimization_barrier((sides, balance_list))
+    low_y, high_y = both_ways(*sides, "gy")
     live = balance_list >= 0
     owner = jnp.where(live, balance_list // OWN_BLK, devices)
     slot = balance_list % OWN_BLK
@@ -397,27 +427,20 @@
         return lax.all_to_all(x, everyone, split_axis=0, concat_axis=0, tiled=True)
 
     outgoing = send_rows(send_source, codes, planes, home_cap, send_cap)
-    outgoing, fields, winds, diffusion, cells = lax.optimization_barrier(
-        (outgoing, fields, winds, diffusion, cells)
+    outgoing, low_y, high_y, fields, winds, diffusion, cells = lax.optimization_barrier(
+        (outgoing, low_y, high_y, fields, winds, diffusion, cells)
     )
     arrived = exchange(outgoing)
 
-    def edge(xs, ys):
+    def edge(xs):
         grids = (fields, winds, diffusion[None])
-        return jnp.concatenate([g[:, xs, ys] for g in grids], axis=0)
-
-    low_x, high_x = both_ways(
-        edge(slice(0, 2), every), edge(slice(width - 2, width), every), "gx"
-    )
-
-    def side(ys):
-        return jnp.concatenate([low_x[:, :, ys], edge(every, ys), high_x[:, :, ys]], axis=1)
-
-    sides = (side(slice(0, strip)), side(slice(merged - strip, merged)))
-    sides, column = lax.optimization_barrier((sides, cells[:, 0] // NZ))
-    low_y, high_y = both_ways(*sides, "gy")
-    low_y = jnp.pad(low_y, ((0, 0), (0, 0), (LANES - strip, 0)))
-    high_y = jnp.pad(high_y, ((0, 0), (0, 0), (0, LANES - strip)))
+        own = jnp.concatenate([g[:, xs] for g in grids], axis=0)
+        return jnp.concatenate([low_y[:, xs], own, high_y[:, xs]], axis=2)
+
+    x_edges = (edge(slice(0, 2)), edge(slice(width - 2, width)))
+    x_edges, cells, fields = lax.optimization_barrier((x_edges, cells, fields))
+    column = cells[:, 0] // NZ
+    low_x, high_x = both_ways(*x_edges, "gx")
 
     level = cells % NZ
     gap = jnp.zeros((column_count, LANES // 2 - NZ), jnp.float32)

time: 124 us -> 108 us (0.87)
  starting transfers between devices: 35.1 us -> 15 us
  waiting for transfers between devices: 12 us -> 22.4 us
  local copies, waits for them, and re-layouts: 20.6 us -> 15.5 us
  other arithmetic: 12.7 us -> 9.93 us
  Pallas kernels: 42.3 us -> 44.2 us
    all_to_all x2, waiting for transfers between devices: 4.13 us -> 22.4 us  [exchange(): return lax.all_to_all(x, everyone, split_axis=0, concat_axis=0, tiled=True)]
    all_to_all x2, starting transfers between devices: 23.9 us -> 7.14 us  [exchange(): return lax.all_to_all(x, everyone, split_axis=0, concat_axis=0, tiled=True)]
    ppermute x2, waiting for transfers between devices: 7.17 us -> 0.01 us  [both_ways(): lax.ppermute(high_edge, axis, [(i, (i + 1) % count) for i in range(count)])]
    slice x8 -> x4, local copies, waits for them, and re-layouts: 7.7 us -> 3.21 us  [the longest x3 3.19 us: edge(): own = jnp.concatenate([g[:, xs] for g in grids], axis=0)]
    pallas_call x0 -> x1, Pallas kernels: none -> 1.83 us  [pack_sides(): pl.pallas_call(pack_kernel, grid=(1,), out_shape=(shape, shape), in_specs...]
    ppermute x2, starting transfers between devices: 6.23 us -> 4.54 us  [both_ways(): lax.ppermute(low_edge, axis, [((i + 1) % count, i) for i in range(count)])]
    ppermute x2, starting transfers between devices: 4.98 us -> 3.3 us  [both_ways(): lax.ppermute(high_edge, axis, [(i, (i + 1) % count) for i in range(count)])]
    pad x2 -> x0, local copies, waits for them, and re-layouts: 1.56 us -> none  [the longest x1 0.84 us: per_device(): low_y = jnp.pad(low_y, ((0, 0), (0, 0), (LANES - strip, 0)))]
  transfers between devices with their start and end apart: 6 -> 6, of which waited for: 5 -> 2; matrix products, arithmetic and copies ran while one was open for 23% -> 22% of each run, Pallas kernels for 28% -> 37%
where the time goes in v4:
time: 108 us
  Pallas kernels  44.2 us (41%)
  waiting for transfers between devices  22.4 us (21%)
  local copies, waits for them, and re-layouts  15.5 us (14%)
  starting transfers between devices  15 us (14%)
  other arithmetic  9.93 us (9%)
    all_to_all x2, waiting for transfers between devices, exchange(): return lax.all_to_all(x, everyone, split_axis=0, concat_axis=0, tiled=True)  22.4 us
    pallas_call x1, Pallas kernels, grow_blocks(): pl.pallas_call(lambda *refs: grow_kernel(home_cap, *refs), out_shape=(jax...  15.1 us
    pallas_call x1, Pallas kernels, advance(): pl.pallas_call(stencil_kernel, out_shape=jax.ShapeDtypeStruct(fields.shap...  13.4 us
    all_to_all x2, starting transfers between devices, exchange(): return lax.all_to_all(x, everyone, split_axis=0, concat_axis=0, tiled=True)  7.14 us
    pallas_call x1, Pallas kernels, send_rows(): pl.pallas_call(lambda *refs: send_kernel(home_cap, send_cap, rows, steps,...  6.27 us
    pallas_call x1, Pallas kernels, place_blocks(): pl.pallas_call(lambda *refs: place_kernel(home_cap, send_cap, rows, *refs...  5.56 us
    ppermute x2, starting transfers between devices, both_ways(): lax.ppermute(low_edge, axis, [((i + 1) % count, i) for i in range(count)])  4.54 us
    ppermute x2, starting transfers between devices, both_ways(): lax.ppermute(high_edge, axis, [(i, (i + 1) % count) for i in range(count)])  3.3 us
  transfers between devices with their start and end apart: 6, of which 2 were waited for; matrix products, arithmetic and copies ran while one was open for 22% of the time, Pallas kernels for 37%

profile of v4, /device:TPU:0, one launch (start us, length us, event | category | flops | bytes accessed | tf_op | source)
XLA Modules:
  0.0 107.8 jit_solution(13789387855981639936)
XLA Ops:
  0.6 0.0 copy-start.6
  0.6 1.8 %pack_sides.1 = (f32[9,48,128]{2,1,0:T(8,128)}, f32[9,48,128]{2,1,0:T(8,128)}) custom-call(f32[5,48,2304]{2,1,0:T(8,128)} %fields_ref, f32[5,48,2304]{2,1,0:T(8,128)} %fields_ref, f32[3,48,2304]{2,1,0:T(8,128)} %winds_ref, f32[3,48,2304]{2,1,0:T(8,128)} %winds_ref, f32[48,2304]{1,0:T(8,128)} %diff_ref, f32[48,2304]{1,0:T(8,128)} %diff_ref), custom_call_target="tpu_custom_call" | custom-call | flops 1024 | bytes 1048576 | tf_op jit(solution)/shard_map/pack_sides/pallas_call | solution.py:48
  2.5 3.0 %collective-permute-start = (f32[9,48,128]{2,1,0:T(8,128)}, f32[9,48,128]{2,1,0:T(8,128)S(1)}, u32[]{:S(2)}, u32[]{:S(2)}) collective-permute-start(f32[9,48,128]{2,1,0:T(8,128)} %get-tuple-element.26), channel_id=1, source_target_pairs={{0,1},{1,2},{2,3},{3,4},{4,5},{5,6},{6,7},{7,0},{8,9},{9,10},{10,1... | collective-permute-start | bytes 663560 | tf_op jit(solution)/shard_map/ppermute | solution.py:393
  5.5 3.0 %collective-permute-start.1 = (f32[9,48,128]{2,1,0:T(8,128)}, f32[9,48,128]{2,1,0:T(8,128)S(1)}, u32[]{:S(2)}, u32[]{:S(2)}) collective-permute-start(f32[9,48,128]{2,1,0:T(8,128)} %get-tuple-element.27), channel_id=1, source_target_pairs={{1,0},{2,1},{3,2},{4,3},{5,4},{6,5},{7,6},{0,7},{9,8},{10,9},{11,1... | collective-permute-start | bytes 663560 | tf_op jit(solution)/shard_map/ppermute | solution.py:394
  8.5 0.0 copy-done.6
  8.5 0.7 convert_reduce_fusion.1
  9.2 0.2 convert_reduce_fusion
  9.5 0.9 select_reduce_fusion
  10.4 0.1 convert_element_type.24
  10.5 0.6 pad.4.refs_1_
  11.1 6.3 %send_rows.1 = f32[5888,128]{1,0:T(8,128)} custom-call(s32[512]{0:T(512)} %get-tuple-element.45.refs_0_.refs_1_, f32[32,128]{1,0:T(8,128)} %pad.4.refs_1_, f32[6144,128]{1,0:T(8,128)} %bitcast.18), custom_call_target="tpu_custom_call" | custom-call | flops 1048576 | bytes 6291456 | tf_op jit(solution)/shard_map/send_rows/pallas_call | solution.py:81
  17.4 0.0 collective-permute-done.low_y
  17.4 0.0 collective-permute-done.1.high_y
  17.4 0.0 copy-start.4
  17.4 4.5 %all-to-all-start = ((f32[32,184,128]{2,1,0:T(8,128)}), f32[32,184,128]{2,1,0:T(8,128)S(1)}, u32[]{:S(2)}, u32[]{:S(2)}) async-start(f32[32,184,128]{2,1,0:T(8,128)} %bitcast.21), calls=%async_computation | async-start | bytes 6029312 | tf_op jit(solution)/shard_map/all_to_all | solution.py:427
  21.9 0.0 copy-done.3
  21.9 0.0 copy-done.4
  22.0 0.9 fusion.7
  22.9 1.1 %fusion.6 = (f32[3,2,2304]{2,1,0:T(2,128)S(1)}, f32[3,2,2304]{2,1,0:T(2,128)S(1)}) fusion(f32[3,48,2304]{2,1,0:T(8,128)} %winds_ref), kind=kLoop, calls=%fused_computation.31 | loop fusion | bytes 221184 | tf_op jit(solution)/shard_map/slice | solution.py:437
  24.0 1.2 %fusion.5 = (f32[5,2,2304]{2,1,0:T(2,128)S(1)}, f32[5,2,2304]{2,1,0:T(2,128)S(1)}) fusion(f32[5,48,2304]{2,1,0:T(8,128)} %fields_ref), kind=kLoop, calls=%fused_computation.30 | loop fusion | bytes 368640 | tf_op jit(solution)/shard_map/slice | solution.py:437
  25.2 0.8 pad_maximum_fusion.2
  25.9 0.8 pad_maximum_fusion.1
  26.7 2.0 %fusion.4 = (f32[1,48,2304]{2,1,0:T(8,128)}, f32[1,48,2304]{2,1,0:T(8,128)S(1)}) fusion(f32[5,48,2304]{2,1,0:T(8,128)} %fields_ref), kind=kLoop, calls=%fused_computation.29 | loop fusion | bytes 1769472 | tf_op jit(solution)/shard_map/slice | solution.py:449
  28.7 2.8 %reshape_squeeze.6 = f32[2304,48]{1,0:T(8,128)} reshape(f32[1,48,2304]{2,1,0:T(8,128)} %get-tuple-element.46) | data formatting | bytes 884736 | tf_op jit(solution)/shard_map/reshape;squeeze | solution.py:449
  31.4 1.8 %reshape_squeeze.7 = f32[2304,48]{1,0:T(8,128)} reshape(f32[1,48,2304]{2,1,0:T(8,128)S(1)} %get-tuple-element.47) | data formatting | bytes 884736 | tf_op jit(solution)/shard_map/reshape;squeeze | solution.py:451
  33.2 1.1 copy.11
  34.3 0.0 copy-start.1
  34.3 0.3 collective-permute-start.2
  34.6 1.5 %collective-permute-start.3 = (f32[9,2,2560]{2,1,0:T(2,128)}, f32[9,2,2560]{2,1,0:T(2,128)}, u32[]{:S(2)}, u32[]{:S(2)}) collective-permute-start(f32[9,2,2560]{2,1,0:T(2,128)} %pad_maximum_fusion.1), channel_id=1, source_target_pairs={{8,0},{16,8},{24,16},{0,24},{9,1},{17,9},{25,17},{1,25},{10,2},{18... | collective-permute-start | bytes 552968 | tf_op jit(solution)/shard_map/ppermute | solution.py:394
  36.1 1.8 %add_select_fusion.refs_4_ = s32[512,128]{1,0:T(8,128)} fusion(s32[512,128]{1,0:T(8,128)} %param.10), kind=kLoop, calls=%fused_computation.8 | loop fusion | flops 393216 | bytes 524288 | tf_op jit(solution)/shard_map/jit(remainder)/select_n | solution.py:445
  37.9 0.1 broadcast_in_dim.61
  38.0 0.0 copy-done.1
  38.0 3.3 %pad_maximum_fusion.refs_3_ = f32[2304,128]{1,0:T(8,128)} fusion(f32[2304,16]{1,0:T(8,128)S(1)} %broadcast_in_dim.61, f32[2304,48]{1,0:T(8,128)} %reshape_squeeze.7, f32[2304,48]{1,0:T(8,128)S(1)} %copy-done.1), kind=kLoop, calls=%fused_computation | loop fusion | flops 884736 | bytes 2211840 | tf_op jit(solution)/shard_map/concatenate | solution.py:447
  41.3 0.6 add_select_fusion.1.refs_0_
  41.9 15.1 %grow_blocks.1 = (f32[2304,128]{1,0:T(8,128)}, f32[512,128]{1,0:T(8,128)}) custom-call(s32[512]{0:T(512)} %add_select_fusion.1.refs_0_, s32[512]{0:T(512)} %get-tuple-element.45.refs_0_.refs_1_, s32[1]{0:T(128)} %bitcast.6.refs_2_, f32[2304,128]{1,0:T(8,128)} %pad_maximum_fusion.refs_3_, s32[512,128]{1,0:T(8,128)} %add_select_fusion.refs_4_, ...), custom_call_target="tpu_custom_call" | custom-call | flops 16777216 | bytes 8388608 | tf_op jit(solution)/shard_map/grow_blocks/pallas_call | solution.py:195
  57.0 2.5 %reshape.46.cond_ref = f32[48,2304]{1,0:T(8,128)} reshape(f32[2304,48]{1,0:T(8,128)} %bitcast.24) | data formatting | bytes 884736 | tf_op jit(solution)/shard_map/reshape | solution.py:457
  59.5 0.0 collective-permute-done.2.low_x
  59.5 0.0 collective-permute-done.3.high_x
  59.5 0.7 copy-done.5
  60.2 13.4 %advance.1 = f32[5,48,2304]{2,1,0:T(8,128)} custom-call(f32[5,48,2304]{2,1,0:T(8,128)} %fields_ref, f32[3,48,2304]{2,1,0:T(8,128)} %winds_ref, f32[48,2304]{1,0:T(8,128)} %diff_ref, f32[9,2,2560]{2,1,0:T(2,128)} %copy-done.5, f32[9,2,2560]{2,1,0:T(2,128)} %collective-permute-done.3.high_x, f32[9,48,128]{2,1,0:T(8,128)} %copy-done.3, ...), custom_call_target="tpu_custom_call" | custom-call | flops 67108864 | bytes 16777216 | tf_op jit(solution)/shard_map/advance/pallas_call | solution.py:374
  73.6 18.5 %all-to-all-done = f32[32,184,128]{2,1,0:T(8,128)S(1)} async-done(((f32[32,184,128]{2,1,0:T(8,128)}), f32[32,184,128]{2,1,0:T(8,128)S(1)}, u32[]{:S(2)}, u32[]{:S(2)}) %all-to-all-start) | async-done | bytes 3014688 | tf_op jit(solution)/shard_map/all_to_all | solution.py:427
  92.0 2.6 %all-to-all-start.1 = ((f32[32,16,128]{2,1,0:T(8,128)}), f32[32,16,128]{2,1,0:T(8,128)S(1)}, u32[]{:S(2)}, u32[]{:S(2)}) async-start(f32[32,16,128]{2,1,0:T(8,128)} %bitcast.9), calls=%async_computation.1 | async-start | bytes 524288 | tf_op jit(solution)/shard_map/all_to_all | solution.py:427
  94.7 0.1 eq.48
  94.8 0.8 select_reduce_fusion.2.refs_0_.source_ref
  95.6 5.6 %place_blocks.1.placed_ref = f32[3072,128]{1,0:T(8,128)} custom-call(s32[256]{0:T(256)} %select_reduce_fusion.2.refs_0_.source_ref, f32[5888,128]{1,0:T(8,128)} %bitcast.20), custom_call_target="tpu_custom_call" | custom-call | flops 1048576 | bytes 5242880 | tf_op jit(solution)/shard_map/place_blocks/pallas_call | solution.py:229
  101.2 4.0 %all-to-all-done.1 = f32[32,16,128]{2,1,0:T(8,128)S(1)} async-done(((f32[32,16,128]{2,1,0:T(8,128)}), f32[32,16,128]{2,1,0:T(8,128)S(1)}, u32[]{:S(2)}, u32[]{:S(2)}) %all-to-all-start.1) | async-done | bytes 262176 | tf_op jit(solution)/shard_map/all_to_all | solution.py:427
  105.1 0.7 copy-done.2
  105.8 2.0 %place_radius.1 = f32[3072,128]{1,0:T(8,128)} custom-call(s32[256]{0:T(256)} %select_reduce_fusion.2.refs_0_.source_ref, f32[512,128]{1,0:T(8,128)} %bitcast.25, f32[3072,128]{1,0:T(8,128)} %place_blocks.1.placed_ref), custom_call_target="tpu_custom_call", output_to_operand_aliasing={{}: (2, {})} | custom-call | flops 65536 | bytes 524288 | tf_op jit(solution)/shard_map/place_radius/pallas_call | solution.py:254
  (12 shorter events, 0.1 us)
Async XLA Ops:
  0.6 7.9 %copy-start.6 = (s32[512]{0:T(512)S(1)}, s32[512]{0:T(512)}, u32[]{:S(2)}) copy-start(s32[512]{0:T(512)} %param.11) | copy-start | bytes 6148
  2.5 14.9 %collective-permute-start = (f32[9,48,128]{2,1,0:T(8,128)}, f32[9,48,128]{2,1,0:T(8,128)S(1)}, u32[]{:S(2)}, u32[]{:S(2)}) collective-permute-start(f32[9,48,128]{2,1,0:T(8,128)} %get-tuple-element.26), channel_id=1, source_target_pairs={{0,1},{1,2},{2,3},{3,4},{4,5},{5,6},{6,7},{7,0},{8,9},{9,10},{10,1... | collective-permute-start | bytes 663560 | tf_op jit(solution)/shard_map/ppermute | solution.py:393
  5.5 11.9 %collective-permute-start.1 = (f32[9,48,128]{2,1,0:T(8,128)}, f32[9,48,128]{2,1,0:T(8,128)S(1)}, u32[]{:S(2)}, u32[]{:S(2)}) collective-permute-start(f32[9,48,128]{2,1,0:T(8,128)} %get-tuple-element.27), channel_id=1, source_target_pairs={{1,0},{2,1},{3,2},{4,3},{5,4},{6,5},{7,6},{0,7},{9,8},{10,9},{11,1... | collective-permute-start | bytes 663560 | tf_op jit(solution)/shard_map/ppermute | solution.py:394
  17.4 4.5 %copy-start.3 = (f32[9,48,128]{2,1,0:T(8,128)}, f32[9,48,128]{2,1,0:T(8,128)S(1)}, u32[]{:S(2)}) copy-start(f32[9,48,128]{2,1,0:T(8,128)S(1)} %collective-permute-done.low_y) | copy-start | bytes 663556
  17.4 4.5 %copy-start.4 = (f32[9,48,128]{2,1,0:T(8,128)}, f32[9,48,128]{2,1,0:T(8,128)S(1)}, u32[]{:S(2)}) copy-start(f32[9,48,128]{2,1,0:T(8,128)S(1)} %collective-permute-done.1.high_y) | copy-start | bytes 663556
  17.4 74.6 %all-to-all-start = ((f32[32,184,128]{2,1,0:T(8,128)}), f32[32,184,128]{2,1,0:T(8,128)S(1)}, u32[]{:S(2)}, u32[]{:S(2)}) async-start(f32[32,184,128]{2,1,0:T(8,128)} %bitcast.21), calls=%async_computation | async-start | bytes 6029312 | tf_op jit(solution)/shard_map/all_to_all | solution.py:427
  34.3 3.7 %copy-start.1 = (f32[2304,48]{1,0:T(8,128)S(1)}, f32[2304,48]{1,0:T(8,128)}, u32[]{:S(2)}) copy-start(f32[2304,48]{1,0:T(8,128)} %reshape_squeeze.6) | copy-start | bytes 1327108
  34.3 25.2 %collective-permute-start.2 = (f32[9,2,2560]{2,1,0:T(2,128)}, f32[9,2,2560]{2,1,0:T(2,128)S(1)}, u32[]{:S(2)}, u32[]{:S(2)}) collective-permute-start(f32[9,2,2560]{2,1,0:T(2,128)} %pad_maximum_fusion.2), channel_id=1, source_target_pairs={{0,8},{8,16},{16,24},{24,0},{1,9},{9,17},{17,25},{25,1},{2,10},{10... | collective-permute-start | bytes 552968 | tf_op jit(solution)/shard_map/ppermute | solution.py:393
  34.6 24.9 %collective-permute-start.3 = (f32[9,2,2560]{2,1,0:T(2,128)}, f32[9,2,2560]{2,1,0:T(2,128)}, u32[]{:S(2)}, u32[]{:S(2)}) collective-permute-start(f32[9,2,2560]{2,1,0:T(2,128)} %pad_maximum_fusion.1), channel_id=1, source_target_pairs={{8,0},{16,8},{24,16},{0,24},{9,1},{17,9},{25,17},{1,25},{10,2},{18... | collective-permute-start | bytes 552968 | tf_op jit(solution)/shard_map/ppermute | solution.py:394
  59.5 0.7 copy-start.5
  92.0 3.5 %copy-start = (f32[32,184,128]{2,1,0:T(8,128)}, f32[32,184,128]{2,1,0:T(8,128)S(1)}, u32[]{:S(2)}) copy-start(f32[32,184,128]{2,1,0:T(8,128)S(1)} %all-to-all-done) | copy-start | bytes 9043972
  92.0 13.1 %all-to-all-start.1 = ((f32[32,16,128]{2,1,0:T(8,128)}), f32[32,16,128]{2,1,0:T(8,128)S(1)}, u32[]{:S(2)}, u32[]{:S(2)}) async-start(f32[32,16,128]{2,1,0:T(8,128)} %bitcast.9), calls=%async_computation.1 | async-start | bytes 524288 | tf_op jit(solution)/shard_map/all_to_all | solution.py:427
  105.1 0.7 copy-start.2
